TPU v7x, 512 devices: a whole 4x8x8 slice. The times are simulated.
512 devices in a mesh: dp: 32 (over y_lo, x, core), expert: 16 (over z, y_hi).
Axes of the slice: x: 4, y: 8 (y_hi: 2, y_lo: 4; y = y_hi * 4 + y_lo), z: 8, core: 2. Of those that a mesh axis runs over, the one named last changes fastest.
Arguments:
- tokens: bfloat16 [65536, 2048], P(('dp', 'expert')), may hold values from -24 to 24
- cotangent: bfloat16 [65536, 2048], P(('dp', 'expert')), may hold values from -6 to 6
- route: int32 [65536, 1], P(('dp', 'expert')), may hold values from 0 to 3; in each aligned block of 128 rows (0 to 127, 128 to 255, ...) at most 48 rows name the same one
- prob: bfloat16 [65536], P(('dp', 'expert')), may hold values from 0.049804688 to 1
- w_gate: float32 [16, 2048, 128], P('expert'), may hold values from -0.125 to 0.125
- w_up: float32 [16, 2048, 128], P('expert'), may hold values from -0.125 to 0.125
- w_down: float32 [16, 2048, 128], P('expert'), may hold values from -0.25 to 0.25
Outputs:
- grad_input: bfloat16 [65536, 2048], P(('dp', 'expert'))
- grad_prob: bfloat16 [65536], P(('dp', 'expert'))
- grad_gate: float32 [16, 2048, 128], P('expert', 'dp')
- grad_up: float32 [16, 2048, 128], P('expert', 'dp')
- grad_down: float32 [16, 2048, 128], P('expert', 'dp')
Inputs may be any that keep to these rules, and one draw needn't show every extreme that they name: `route`: within each device's aligned block of 128 rows (devices in the order of dp, then expert) each hot expert is named by at most 48 rows, a bound that some block reaches.
All inputs are finite; a program needn't handle non-finite values.
Results may differ from a plain program's by a relative error of at most 0.003.
Values may be sent and summed in bfloat16 or wider, within the bound.
A program may use at most 128 MiB of HBM per device.

v0:
```python
import math

import jax
import jax.numpy as jnp
from jax import lax
from jax.sharding import PartitionSpec as P

D = 2048
HOT = 4
CAP = 48


highest = lax.Precision.HIGHEST


def expert_rows(row_tokens, row_cotangents, row_probs, gate_weight, up_weight, down_weight):
    probs_f32 = row_probs.astype(jnp.float32)
    gate_pre = jnp.dot(
        row_tokens, gate_weight, precision=highest, preferred_element_type=jnp.float32
    )
    up_pre = jnp.dot(row_tokens, up_weight, precision=highest, preferred_element_type=jnp.float32)
    sigmoid_val = jax.nn.sigmoid(gate_pre)
    activation = gate_pre * sigmoid_val
    hidden = activation * up_pre
    backward = jnp.dot(
        row_cotangents, down_weight, precision=highest, preferred_element_type=jnp.float32
    )
    prob_part = jnp.sum(hidden * backward, axis=1)
    d_hidden = probs_f32[:, None] * backward
    d_up = d_hidden * activation
    d_gate = d_hidden * up_pre * sigmoid_val * (1.0 + gate_pre * (1.0 - sigmoid_val))
    input_part = jnp.dot(d_gate, gate_weight.T, precision=highest) + jnp.dot(
        d_up, up_weight.T, precision=highest
    )
    grad_g = jnp.dot(row_tokens.T, d_gate, precision=highest, preferred_element_type=jnp.float32)
    grad_u = jnp.dot(row_tokens.T, d_up, precision=highest, preferred_element_type=jnp.float32)
    scaled_cot = probs_f32[:, None] * row_cotangents
    grad_d = jnp.dot(scaled_cot.T, hidden, precision=highest)
    return (input_part, prob_part, grad_g, grad_u, grad_d)


def slot_positions(route_column):
    onehot = (route_column[:, None] == jnp.arange(HOT, dtype=jnp.int32)[None, :]).astype(jnp.int32)
    earlier = jnp.cumsum(onehot, axis=0) - onehot
    rank_in_expert = jnp.sum(earlier * onehot, axis=1)
    return route_column * CAP + rank_in_expert


def shards(tokens, cotangent, route, prob, w_gate, w_up, w_down):
    quarters = lax.axis_size("expert") // HOT
    position = slot_positions(route[:, 0])
    placing = (jnp.arange(HOT * CAP, dtype=jnp.int32)[:, None] == position[None, :]).astype(
        jnp.bfloat16
    )
    slot_tok = jnp.dot(placing, tokens, preferred_element_type=jnp.float32).astype(jnp.bfloat16)
    slot_cot = jnp.dot(placing, cotangent, preferred_element_type=jnp.float32).astype(jnp.bfloat16)
    slot_prob = jnp.zeros((HOT * CAP,), jnp.bfloat16).at[position].set(prob)
    gate_weight = w_gate[0]
    up_weight = w_up[0]
    down_weight = w_down[0]
    send_tok = jnp.repeat(slot_tok.reshape(HOT, CAP, D), quarters, axis=0)
    send_cot = jnp.repeat(slot_cot.reshape(HOT, CAP, D), quarters, axis=0)
    send_prob = jnp.repeat(slot_prob.reshape(HOT, CAP), quarters, axis=0)
    recv_tok, recv_cot, recv_prob = (
        lax.all_to_all(send_tok, "expert", split_axis=0, concat_axis=0, tiled=True),
        lax.all_to_all(send_cot, "expert", split_axis=0, concat_axis=0, tiled=True),
        lax.all_to_all(send_prob, "expert", split_axis=0, concat_axis=0, tiled=True),
    )
    sources = recv_tok.shape[0]
    input_part, prob_part, grad_g, grad_u, grad_d = expert_rows(
        recv_tok.reshape(sources * CAP, D),
        recv_cot.reshape(sources * CAP, D),
        recv_prob.reshape(sources * CAP),
        gate_weight,
        up_weight,
        down_weight,
    )
    back_input, back_prob = (
        lax.all_to_all(
            input_part.reshape(sources, CAP, D), "expert", split_axis=0, concat_axis=0, tiled=True
        ),
        lax.all_to_all(
            prob_part.reshape(sources, CAP), "expert", split_axis=0, concat_axis=0, tiled=True
        ),
    )
    summed_input = (
        jnp.sum(back_input.reshape(HOT, quarters, CAP, D), axis=1)
        .astype(jnp.bfloat16)
        .reshape(HOT * CAP, D)
    )
    summed_prob = (
        jnp.sum(back_prob.reshape(HOT, quarters, CAP), axis=1)
        .astype(jnp.bfloat16)
        .reshape(HOT * CAP)
    )
    grad_input = summed_input[position]
    grad_prob = summed_prob[position]
    stacked = jnp.stack([grad_g, grad_u, grad_d])
    reduced = lax.psum_scatter(stacked, "dp", scatter_dimension=1, tiled=True)
    token_total = tokens.shape[0] * lax.axis_size("dp") * lax.axis_size("expert")
    reduced = reduced * (1.0 / math.sqrt(token_total))
    return (grad_input, grad_prob, reduced[0][None], reduced[1][None], reduced[2][None])


def solution(mesh):
    placed = (
        P(("dp", "expert"), None),
        P(("dp", "expert"), None),
        P(("dp", "expert"), None),
        P(("dp", "expert")),
        P("expert", None, None),
        P("expert", None, None),
        P("expert", None, None),
    )
    return jax.shard_map(
        shards,
        mesh=mesh,
        in_specs=placed,
        out_specs=(
            P(("dp", "expert"), None),
            P(("dp", "expert")),
            P("expert", "dp", None),
            P("expert", "dp", None),
            P("expert", "dp", None),
        ),
        check_vma=False,
    )
```

profile of v0, /device:TPU:1, one launch (start us, length us, event | category | flops | bytes accessed | tf_op | source)
XLA Modules:
  0.0 715.2 jit_solution(14756488110416962843)
XLA Ops:
  7.2 0.8 fusion.18
  8.2 0.8 select_reduce_fusion
  9.0 0.7 fusion.21
  9.7 1.5 scatter_custom_fusion
  11.9 16.2 %all-to-all-start = ((bf16[16,1,48]{2,1,0:T(2,128)(2,1)}), bf16[16,1,48]{2,1,0:T(2,128)(2,1)S(1)}, u32[]{:S(2)}, u32[]{:S(2)}) async-start(bf16[16,1,48]{2,1,0:T(2,128)(2,1)} %copy.14), calls=%async_computation | async-start | bytes 16384 | tf_op jit(solution)/shard_map/all_to_all | solution.py:67
  28.1 0.7 multiply_add_fusion
  28.8 1.4 convolution_convert_fusion
  30.2 9.1 %all-to-all-done = bf16[16,1,48]{2,1,0:T(2,128)(2,1)S(1)} async-done(((bf16[16,1,48]{2,1,0:T(2,128)(2,1)}), bf16[16,1,48]{2,1,0:T(2,128)(2,1)S(1)}, u32[]{:S(2)}, u32[]{:S(2)}) %all-to-all-start) | async-done | bytes 1568 | tf_op jit(solution)/shard_map/all_to_all | solution.py:67
  39.3 2.1 broadcast_in_dim.11
  41.4 4.6 all-to-all-start.2
  46.4 80.2 %all-to-all-done.2 = bf16[16,48,2048]{2,1,0:T(8,128)(2,1)} async-done(((bf16[16,48,2048]{2,1,0:T(8,128)(2,1)}), bf16[16,48,2048]{2,1,0:T(8,128)(2,1)}, u32[]{:S(2)}, u32[]{:S(2)}) %all-to-all-start.2) | async-done | bytes 3145760 | tf_op jit(solution)/shard_map/all_to_all | solution.py:65
  126.5 2.1 broadcast_in_dim.10
  128.6 10.6 %all-to-all-start.1 = ((bf16[16,48,2048]{2,1,0:T(8,128)(2,1)}), bf16[16,48,2048]{2,1,0:T(8,128)(2,1)}, u32[]{:S(2)}, u32[]{:S(2)}) async-start(bf16[16,48,2048]{2,1,0:T(8,128)(2,1)} %bitcast.53), calls=%async_computation.1 | async-start | bytes 6291456 | tf_op jit(solution)/shard_map/all_to_all | solution.py:66
  139.3 4.6 fusion.9
  143.9 5.3 fusion.12
  149.1 69.3 %all-to-all-done.1 = bf16[16,48,2048]{2,1,0:T(8,128)(2,1)} async-done(((bf16[16,48,2048]{2,1,0:T(8,128)(2,1)}), bf16[16,48,2048]{2,1,0:T(8,128)(2,1)}, u32[]{:S(2)}, u32[]{:S(2)}) %all-to-all-start.1) | async-done | bytes 3145760 | tf_op jit(solution)/shard_map/all_to_all | solution.py:66
  218.4 4.9 multiply_reduce_fusion
  223.3 0.7 all_to_all.26
  224.0 10.4 %all-to-all-start.4 = ((f32[16,1,48]{2,1,0:T(1,128)}), f32[16,1,48]{2,1,0:T(1,128)S(1)}, u32[]{:S(2)}, u32[]{:S(2)}) async-start(f32[16,1,48]{2,1,0:T(1,128)} %all_to_all.26), calls=%async_computation.4 | async-start | bytes 16384 | tf_op jit(solution)/shard_map/all_to_all | solution.py:82
  234.4 5.4 fusion.7
  239.8 7.4 %convolution_add_fusion = f32[768,2048]{1,0:T(8,128)} fusion(f32[768,2048]{1,0:T(8,128)S(1)} %fusion.7, f32[1,2048,128]{2,1,0:T(8,128)S(1)} %copy-done.1, f32[768,128]{0,1:T(8,128)S(1)} %get-tuple-element.10, f32[768]{0:T(1024)S(1)} %reshape.83, f32[768,128]{0,1:T(8,128)S(1)} %fusion.9), kind=kOutput, calls=%fused_computation.7 | convolution fusion | flops 2418081792 | bytes 14420992 | tf_op jit(solution)/shard_map/dot_general | solution.py:32
  247.2 11.6 %all-to-all-start.3 = ((f32[16,48,2048]{2,1,0:T(8,128)}), f32[16,48,2048]{2,1,0:T(8,128)}, u32[]{:S(2)}, u32[]{:S(2)}) async-start(f32[16,48,2048]{2,1,0:T(8,128)} %bitcast.52), calls=%async_computation.3 | async-start | bytes 12582912 | tf_op jit(solution)/shard_map/all_to_all | solution.py:79
  259.1 5.3 convolution_bitcast_fusion.1
  264.4 5.5 convolution_bitcast_fusion
  269.9 12.5 %fusion.4 = f32[1,2048,128]{2,1,0:T(8,128)S(1)} fusion(bf16[768,2048]{1,0:T(8,128)(2,1)} %bitcast.6, f32[768]{0:T(1024)S(1)} %reshape.83, f32[768,128]{0,1:T(8,128)S(1)} %copy-done.2, f32[768,128]{0,1:T(8,128)S(1)} %fusion.9), kind=kOutput, calls=%fused_computation.12 | convolution fusion | flops 2419556352 | bytes 4983808 | tf_op jit(solution)/shard_map/dot_general | solution.py:38
  282.4 1.9 pad_maximum_fusion
  284.4 1.7 gather_fusion.1
  286.2 414.9 %reduce-scatter.2.cloned.1.call-done = f32[3,64,128]{2,1,0:T(8,128)} async-done(((f32[3,2048,128]{2,1,0:T(8,128)}), f32[3,64,128]{2,1,0:T(8,128)}) %reduce-scatter.2.cloned.1.call-update) | async-done | bytes 98320 | tf_op jit(solution)/shard_map/reduce_scatter | solution.py:99
  701.0 0.9 broadcast_multiply_fusion
  701.9 0.6 fusion.27
  702.6 3.6 bitcast_reduce_fusion
  706.1 1.7 gather_fusion
  (22 shorter events, 1.7 us)
Async XLA Ops:
  7.2 132.1 %copy-start = (f32[1,2048,128]{2,1,0:T(8,128)S(1)}, f32[1,2048,128]{2,1,0:T(8,128)}, u32[]{:S(2)}) copy-start(f32[1,2048,128]{2,1,0:T(8,128)} %param.11) | copy-start | bytes 3145732
  11.9 27.4 %all-to-all-start = ((bf16[16,1,48]{2,1,0:T(2,128)(2,1)}), bf16[16,1,48]{2,1,0:T(2,128)(2,1)S(1)}, u32[]{:S(2)}, u32[]{:S(2)}) async-start(bf16[16,1,48]{2,1,0:T(2,128)(2,1)} %copy.14), calls=%async_computation | async-start | bytes 16384 | tf_op jit(solution)/shard_map/all_to_all | solution.py:67
  41.3 4.6 copy-start.3
  41.4 85.2 %all-to-all-start.2 = ((bf16[16,48,2048]{2,1,0:T(8,128)(2,1)}), bf16[16,48,2048]{2,1,0:T(8,128)(2,1)}, u32[]{:S(2)}, u32[]{:S(2)}) async-start(bf16[16,48,2048]{2,1,0:T(8,128)(2,1)} %bitcast.54), calls=%async_computation.2 | async-start | bytes 6291456 | tf_op jit(solution)/shard_map/all_to_all | solution.py:65
  128.6 89.8 %all-to-all-start.1 = ((bf16[16,48,2048]{2,1,0:T(8,128)(2,1)}), bf16[16,48,2048]{2,1,0:T(8,128)(2,1)}, u32[]{:S(2)}, u32[]{:S(2)}) async-start(bf16[16,48,2048]{2,1,0:T(8,128)(2,1)} %bitcast.53), calls=%async_computation.1 | async-start | bytes 6291456 | tf_op jit(solution)/shard_map/all_to_all | solution.py:66
  139.2 4.7 copy-start.1
  224.0 23.2 %all-to-all-start.4 = ((f32[16,1,48]{2,1,0:T(1,128)}), f32[16,1,48]{2,1,0:T(1,128)S(1)}, u32[]{:S(2)}, u32[]{:S(2)}) async-start(f32[16,1,48]{2,1,0:T(1,128)} %all_to_all.26), calls=%async_computation.4 | async-start | bytes 16384 | tf_op jit(solution)/shard_map/all_to_all | solution.py:82
  247.2 455.3 %all-to-all-start.3 = ((f32[16,48,2048]{2,1,0:T(8,128)}), f32[16,48,2048]{2,1,0:T(8,128)}, u32[]{:S(2)}, u32[]{:S(2)}) async-start(f32[16,48,2048]{2,1,0:T(8,128)} %bitcast.52), calls=%async_computation.3 | async-start | bytes 12582912 | tf_op jit(solution)/shard_map/all_to_all | solution.py:79
  258.9 442.2 %reduce-scatter.2.cloned.1.call-start = ((), (), s32[]{:S(2)}) async-start(), calls=%async_computation.6 | async-start | bytes 3244032 | tf_op jit(solution)/shard_map/reduce_scatter | solution.py:99
  264.4 5.5 copy-start.2
Sparse Core Ops, SparseCore 0:
  284.4 416.5 reduce-scatter.1
where the time goes:
time: 727 us; the launch traced here: 715 us
  waiting for transfers between devices  573 us (79%)
  starting transfers between devices  53.7 us (7%)
  matrix products  52.6 us (7%)
  between operations  14.7 us (2%)
  local copies, waits for them, and re-layouts  11.2 us (2%)
  other arithmetic  9.56 us (1%)
    reduce_scatter x1, waiting for transfers between devices, shards(): reduced = lax.psum_scatter(stacked, 'dp', scatter_dimension=1, tiled=True)  415 us
    all_to_all x1, waiting for transfers between devices, shards(): lax.all_to_all(send_tok, 'expert', split_axis=0, concat_axis=0, tiled=True)  80.2 us
    all_to_all x1, waiting for transfers between devices, shards(): lax.all_to_all(send_cot, 'expert', split_axis=0, concat_axis=0, tiled=True)  69.3 us
    all_to_all x1, starting transfers between devices, shards(): lax.all_to_all(send_prob, 'expert', split_axis=0, concat_axis=0, tiled=True)  16.2 us
  transfers between devices with their start and end apart: 6, of which 4 were waited for; matrix products, arithmetic and copies ran while one was open for 8% of the time, Pallas kernels for 0%

commit v1 on v0

v1 whole, which is shorter than its diff:
```python
import math

import jax
import jax.numpy as jnp
from jax import lax
from jax.experimental import pallas as pl
from jax.experimental.pallas import tpu as pltpu
from jax.sharding import PartitionSpec as P

D = 2048
HOT = 4
CAP = 48
FQ = 128
NX, NYL, NYH, NZ, NC = 4, 4, 2, 8, 2
NY = NYL * NYH
EXTRA = 128
WIDE = D + EXTRA
W_TOP = 32767.0
MESH = pl.DeviceIdType.MESH
f32, bf16, i32 = jnp.float32, jnp.bfloat16, jnp.int32


def coords():
    dp = lax.axis_index("dp")
    ex = lax.axis_index("expert")
    core = lax.rem(dp, NC)
    x = lax.rem(lax.div(dp, NC), NX)
    ylo = lax.div(dp, NC * NX)
    yhi = lax.rem(ex, NYH)
    z = lax.div(ex, NYH)
    return x, yhi * NYL + ylo, z, core


def device(x, y, z, core):
    return ((lax.rem(y, NYL) * NX + x) * NC + core, z * NYH + lax.div(y, NYL))


def slot_route(z, k):
    odd = lax.rem(z, 2)
    sign = 1 - 2 * odd
    to = sign * (k if k % 2 == 0 else -k)
    come = sign * -k
    return lax.rem(z + to + NZ, NZ), lax.rem(z + come + NZ, NZ)


def remote(src, dst, send, recv, dev):
    return pltpu.make_async_remote_copy(
        src_ref=src, dst_ref=dst, send_sem=send, recv_sem=recv, device_id=dev, device_id_type=MESH
    )


def enter(sources, count):
    barrier = pltpu.get_barrier_semaphore()
    for dev in sources:
        pl.semaphore_signal(barrier, inc=1, device_id=dev, device_id_type=MESH)
    pl.semaphore_wait(barrier, count)


def gather_kernel(tok_ref, cot_ref, w_ref, s_ref, rtok_ref, rcot_ref, wall_ref, sall_ref,
                  s_send, s_recv, ds_send, ds_recv, z_send, z_recv, y_send, y_recv, x_send, x_recv, c_send, c_recv, loc):
    x, y, z, c = coords()
    ylo, yhi = lax.rem(y, NYL), lax.div(y, NYL)
    zlo = lax.rem(z, 2)
    zp = z + 1 - 2 * zlo
    right, left = lax.rem(x + 1, NX), lax.rem(x + NX - 1, NX)
    routes = [slot_route(z, k) for k in (1, 2, 3)]
    ys = [lax.rem(y + j, NY) for j in range(1, NY)]
    enter(
        [device(x, y, come, c) for _, come in routes]
        + [device(x, y, zp, c)]
        + [device(x, yy, z, c) for yy in ys]
        + [device(right, y, z, c), device(left, y, z, c), device(x, y, z, 1 - c)],
        3 + 1 + 7 + 2 + 1,
    )
    row = pl.multiple_of(((c * NX + x) * NYL + ylo) * 32, 32)
    quarter = yhi * 2 + zlo
    mine = pl.ds(quarter * 3, 3)
    zc = remote(w_ref, wall_ref.at[mine, pl.ds(row, 32), :], z_send, z_recv, device(x, y, zp, c))
    zc.start()
    sz = remote(s_ref, sall_ref.at[quarter], s_send.at[0], s_recv.at[0], device(x, y, zp, c))
    sz.start()
    own = pltpu.make_async_copy(w_ref, wall_ref.at[mine, pl.ds(row, 32), :], loc.at[0])
    own.start()
    own_s = pltpu.make_async_copy(s_ref, sall_ref.at[quarter], loc.at[3])
    own_s.start()
    tokens = []
    for i, k in enumerate((1, 2, 3)):
        dev = device(x, y, routes[i][0], c)
        for j, (src, dst) in enumerate(((tok_ref, rtok_ref), (cot_ref, rcot_ref))):
            copy = remote(src.at[k], dst.at[k], ds_send.at[i, j], ds_recv.at[i, j], dev)
            copy.start()
            tokens.append(copy)
    own_tok = pltpu.make_async_copy(tok_ref.at[0], rtok_ref.at[0], loc.at[1])
    own_cot = pltpu.make_async_copy(cot_ref.at[0], rcot_ref.at[0], loc.at[2])
    own_tok.start()
    own_cot.start()
    own.wait()
    zc.wait()
    own_s.wait()
    sz.wait()
    block = wall_ref.at[pl.ds(yhi * 6, 6), pl.ds(row, 32), :]
    ycs = []
    for j in range(1, NY):
        copy = remote(block, block, y_send.at[j - 1], y_recv.at[j - 1], device(x, ys[j - 1], z, c))
        copy.start()
        ycs.append(copy)
    pair = sall_ref.at[pl.ds(yhi * 2, 2)]
    sy = remote(pair, pair, s_send.at[1], s_recv.at[1], device(x, ys[3], z, c))
    sy.start()
    for copy in ycs:
        copy.wait()
    sy.wait()

    def part(xx, half):
        start = pl.multiple_of((c * NX + xx) * 128, 128)
        if half is None:
            return wall_ref.at[:, pl.ds(start, 128), :]
        return wall_ref.at[pl.ds(half * 6, 6), pl.ds(start, 128), :]

    to_right = remote(part(x, None), part(x, None), x_send.at[0], x_recv.at[0], device(right, y, z, c))
    to_left = remote(part(x, None), part(x, None), x_send.at[1], x_recv.at[1], device(left, y, z, c))
    to_right.start()
    to_left.start()
    to_right.wait_recv()
    on_right = remote(part(left, 0), part(left, 0), x_send.at[2], x_recv.at[2], device(right, y, z, c))
    on_right.start()
    to_left.wait_recv()
    on_left = remote(part(right, 1), part(right, 1), x_send.at[3], x_recv.at[3], device(left, y, z, c))
    on_left.start()
    on_right.wait_recv()
    on_left.wait_recv()
    half = wall_ref.at[:, pl.ds(pl.multiple_of(c * 512, 512), 512), :]
    cc = remote(half, half, c_send, c_recv, device(x, y, z, 1 - c))
    cc.start()
    for copy in (to_right, to_left, on_right, on_left):
        copy.wait_send()
    cc.wait()
    for copy in tokens:
        copy.wait()
    own_tok.wait()
    own_cot.wait()


def gather(slot_tok, slot_cot, w_chunk, scales):
    vmem = pl.BlockSpec(memory_space=pltpu.VMEM)
    anyspace = pl.BlockSpec(memory_space=pl.ANY)
    dma = pltpu.SemaphoreType.DMA
    return pl.pallas_call(
        gather_kernel,
        out_shape=[
            jax.ShapeDtypeStruct(slot_tok.shape, slot_tok.dtype),
            jax.ShapeDtypeStruct(slot_cot.shape, slot_cot.dtype),
            jax.ShapeDtypeStruct((12, D // 2, FQ), w_chunk.dtype),
            jax.ShapeDtypeStruct((4, 8, FQ), f32),
        ],
        in_specs=[vmem] * 4,
        out_specs=[anyspace] * 4,
        scratch_shapes=[dma((2,)), dma((2,)), dma((3, 2)), dma((3, 2)), dma, dma, dma((7,)), dma((7,)), dma((4,)), dma((4,)), dma, dma,
                        dma((4,))],
        compiler_params=pltpu.CompilerParams(collective_id=0, has_side_effects=True),
    )(slot_tok, slot_cot, w_chunk, scales)


def scatter_kernel(dx_ref, g_ref, back_ref, out_ref,
                   c_in, x_out, x_in, x_mid, y_out, y_in, z_out, z_in, gbuf,
                   r_send, r_recv, c_send, c_recv, x_send, x_recv, y_send, y_recv, z_send, z_recv, loc):
    x, y, z, c = coords()
    ylo, yhi = lax.rem(y, NYL), lax.div(y, NYL)
    zlo = lax.rem(z, 2)
    zp = z + 1 - 2 * zlo
    right, left = lax.rem(x + 1, NX), lax.rem(x + NX - 1, NX)
    far = lax.rem(x + 2, NX)
    routes = [slot_route(z, k) for k in (1, 2, 3)]
    ys = [lax.rem(y + j, NY) for j in range(1, NY)]
    enter(
        [device(x, y, to, c) for to, _ in routes]
        + [device(x, y, zp, c)]
        + [device(x, yy, z, c) for yy in ys]
        + [device(right, y, z, c), device(left, y, z, c), device(x, y, z, 1 - c)],
        3 + 1 + 7 + 2 + 1,
    )
    cc = remote(g_ref.at[:, 1 - c], c_in, c_send, c_recv, device(x, y, z, 1 - c))
    cc.start()
    mine = pltpu.make_async_copy(g_ref.at[:, c], gbuf, loc.at[0])
    mine.start()
    returns = []
    for i, k in enumerate((1, 2, 3)):
        copy = remote(dx_ref.at[k], back_ref.at[k], r_send.at[i], r_recv.at[i], device(x, y, routes[i][1], c))
        copy.start()
        returns.append(copy)
    own = pltpu.make_async_copy(dx_ref.at[0], back_ref.at[0], loc.at[1])
    own.start()
    mine.wait()
    cc.wait()
    acc = lambda g, xx: gbuf[g * NX + xx] + c_in[g * NX + xx]

    def fill_far(g, _):
        x_out[0, g] = acc(g, far).astype(bf16)
        return 0

    lax.fori_loop(0, 48, fill_far, 0)
    far_right = remote(x_out.at[0, pl.ds(0, 24)], x_mid.at[pl.ds(0, 24)], x_send.at[0], x_recv.at[0],
                       device(right, y, z, c))
    far_left = remote(x_out.at[0, pl.ds(24, 24)], x_mid.at[pl.ds(24, 24)], x_send.at[1], x_recv.at[1],
                      device(left, y, z, c))
    far_right.start()
    far_left.start()

    def fill_plain(g, _):
        x_out[2, g] = acc(24 + g, right).astype(bf16)
        x_out[3, g] = acc(g, left).astype(bf16)
        return 0

    lax.fori_loop(0, 24, fill_plain, 0)
    plain_right = remote(x_out.at[2, pl.ds(0, 24)], x_in.at[0, pl.ds(24, 24)], x_send.at[2], x_recv.at[2],
                         device(right, y, z, c))
    plain_left = remote(x_out.at[3, pl.ds(0, 24)], x_in.at[1, pl.ds(0, 24)], x_send.at[3], x_recv.at[3],
                        device(left, y, z, c))
    plain_right.start()
    plain_left.start()
    far_right.wait_recv()
    far_left.wait_recv()

    def fill_near(g, _):
        x_out[1, g] = (acc(g, right) + x_mid[g].astype(f32)).astype(bf16)
        x_out[1, 24 + g] = (acc(24 + g, left) + x_mid[24 + g].astype(f32)).astype(bf16)
        return 0

    lax.fori_loop(0, 24, fill_near, 0)
    sum_right = remote(x_out.at[1, pl.ds(0, 24)], x_in.at[0, pl.ds(0, 24)], x_send.at[4], x_recv.at[4],
                       device(right, y, z, c))
    sum_left = remote(x_out.at[1, pl.ds(24, 24)], x_in.at[1, pl.ds(24, 24)], x_send.at[5], x_recv.at[5],
                      device(left, y, z, c))
    sum_right.start()
    sum_left.start()
    for copy in (plain_right, plain_left, sum_right, sum_left):
        copy.wait_recv()

    def fill_y(g, _):
        total = acc(g, x) + x_in[0, g].astype(f32) + x_in[1, g].astype(f32)
        gbuf[g * NX + x] = total
        y_out[lax.div(g, 24), lax.rem(lax.div(g, 4), 6), lax.rem(g, 4)] = total.astype(bf16)
        return 0

    lax.fori_loop(0, 48, fill_y, 0)
    ycs = []
    for j in range(1, NY):
        yy = ys[j - 1]
        copy = remote(y_out.at[lax.div(yy, NYL), :, lax.rem(yy, NYL)], y_in.at[j - 1], y_send.at[j - 1],
                      y_recv.at[j - 1], device(x, yy, z, c))
        copy.start()
        ycs.append(copy)
    for copy in ycs:
        copy.wait_recv()

    def fill_z(g, _):
        total = gbuf[((yhi * 6 + g) * NYL + ylo) * NX + x]
        for j in range(NY - 1):
            total = total + y_in[j, g].astype(f32)
        z_out[lax.div(g, 3), lax.rem(g, 3)] = total
        return 0

    lax.fori_loop(0, 6, fill_z, 0)
    zc = remote(z_out.at[1 - zlo], z_in, z_send, z_recv, device(x, y, zp, c))
    zc.start()
    zc.wait_recv()
    scale = 1.0 / math.sqrt(NX * NY * NZ * NC * 128)
    for m in range(3):
        out_ref[m] = (z_out[zlo, m] + z_in[m]) * scale
    for copy in returns:
        copy.wait()
    own.wait()
    zc.wait_send()
    for copy in ycs + [far_right, far_left, plain_right, plain_left, sum_right, sum_left]:
        copy.wait_send()


def scatter(dx, grads):
    vmem = pl.BlockSpec(memory_space=pltpu.VMEM)
    anyspace = pl.BlockSpec(memory_space=pl.ANY)
    dma = pltpu.SemaphoreType.DMA
    return pl.pallas_call(
        scatter_kernel,
        out_shape=[
            jax.ShapeDtypeStruct(dx.shape, dx.dtype),
            jax.ShapeDtypeStruct((3, 64, FQ), f32),
        ],
        in_specs=[vmem, anyspace],
        out_specs=[anyspace, vmem],
        scratch_shapes=[
            pltpu.VMEM((192, 64, FQ), f32),
            pltpu.VMEM((4, 48, 64, FQ), bf16),
            pltpu.VMEM((2, 48, 64, FQ), bf16),
            pltpu.VMEM((48, 64, FQ), bf16),
            pltpu.VMEM((2, 6, 4, 64, FQ), bf16),
            pltpu.VMEM((7, 6, 64, FQ), bf16),
            pltpu.VMEM((2, 3, 64, FQ), f32),
            pltpu.VMEM((3, 64, FQ), f32),
            pltpu.VMEM((192, 64, FQ), f32),
            dma((3,)), dma((3,)), dma, dma, dma((6,)), dma((6,)), dma((7,)), dma((7,)), dma, dma, dma((2,)),
        ],
        compiler_params=pltpu.CompilerParams(
            collective_id=1, has_side_effects=True, vmem_limit_bytes=48 * 1024 * 1024
        ),
    )(dx, grads)


def split(v):
    hi = lax.reduce_precision(v, 8, 7)
    return hi.astype(bf16), (v - hi).astype(bf16)


def dot(a, b, dims):
    return lax.dot_general(a, b, (dims, ((), ())), preferred_element_type=f32)


def shards(tokens, cotangent, route, prob, w_gate, w_up, w_down):
    x, y, z, c = coords()
    odd = lax.rem(z, 2)
    turn = lax.rem(route[:, 0] - lax.div(z, 2) + HOT, HOT)
    slot = jnp.where(turn == 0, 0, jnp.where(turn == 1, 2 - odd, jnp.where(turn == 2, 3, 1 + odd)))
    onehot = (slot[:, None] == jnp.arange(HOT, dtype=jnp.int32)[None, :]).astype(f32)
    before = (jnp.arange(128)[:, None] > jnp.arange(128)[None, :]).astype(bf16)
    earlier = jnp.dot(before, onehot.astype(bf16), preferred_element_type=f32)
    rank = jnp.sum(earlier * onehot, axis=1).astype(jnp.int32)
    position = slot * CAP + rank
    placing = (jnp.arange(HOT * CAP, dtype=jnp.int32)[:, None] == position[None, :]).astype(bf16)
    taking = (position[:, None] == jnp.arange(HOT * CAP, dtype=jnp.int32)[None, :]).astype(bf16)
    wide = jnp.concatenate([tokens, jnp.broadcast_to(prob[:, None], (128, EXTRA))], axis=1)
    slot_tok = jnp.dot(placing, wide, preferred_element_type=f32).astype(bf16).reshape(HOT, CAP, WIDE)
    slot_cot = jnp.dot(placing, cotangent, preferred_element_type=f32).astype(bf16).reshape(HOT, CAP, D)
    row = ((c * NX + x) * NYL + lax.rem(y, NYL)) * 32
    tops = [jnp.maximum(jnp.max(jnp.abs(w[0]), axis=0), 1e-30) for w in (w_gate, w_up, w_down)]
    steps = jnp.stack([t * (1.0 / W_TOP) for t in tops])
    chunk = jnp.stack([lax.dynamic_slice(w[0].reshape(2, D // 2, FQ), (0, row, 0), (2, 32, FQ))
                       for w in (w_gate, w_up, w_down)])
    units = jnp.clip(jnp.round(chunk / steps[:, None, None, :]), -W_TOP, W_TOP).astype(i32)
    packed = units[:, 0] * 65536 + (units[:, 1] + 32768)
    rtok, rcot, wall, sall = gather(slot_tok, slot_cot, packed, jnp.pad(steps, ((0, 5), (0, 0))))

    rows = HOT * CAP
    rtok = rtok.reshape(rows, WIDE)
    toks, probs = rtok[:, :D], rtok[:, D:D + 1].astype(f32)
    cots = rcot.reshape(rows, D)
    wall = wall.reshape(4, 3, D // 2, FQ).transpose(1, 2, 0, 3).reshape(3, D // 2, 4 * FQ)
    full = jnp.concatenate([wall >> 16, (wall & 65535) - 32768], axis=1).astype(f32)
    hi, lo = split(full)
    step = sall[:, :3].transpose(1, 0, 2).reshape(3, 1, 4 * FQ)
    ahead = ((1,), (0,))
    gate_pre = (dot(toks, hi[0], ahead) + dot(toks, lo[0], ahead)) * step[0]
    up_pre = (dot(toks, hi[1], ahead) + dot(toks, lo[1], ahead)) * step[1]
    backward = (dot(cots, hi[2], ahead) + dot(cots, lo[2], ahead)) * step[2]
    sig = jax.nn.sigmoid(gate_pre)
    act = gate_pre * sig
    hidden = act * up_pre
    grad_prob = jnp.sum(hidden * backward, axis=1, keepdims=True)
    d_hidden = probs * backward
    d_up = d_hidden * act
    d_gate = d_hidden * up_pre * sig * (1.0 + gate_pre * (1.0 - sig))
    gh, gl = split(d_gate)
    uh, ul = split(d_up)
    hh, hl = split(probs * hidden)
    turned = ((1,), (1,))
    sgh, sgl = split(d_gate * step[0])
    suh, sul = split(d_up * step[1])
    dx = (
        dot(sgh, hi[0], turned) + dot(sgh, lo[0], turned) + dot(sgl, hi[0], turned)
        + dot(suh, hi[1], turned) + dot(suh, lo[1], turned) + dot(sul, hi[1], turned)
    )
    dx = jnp.concatenate([dx, jnp.broadcast_to(grad_prob, (rows, EXTRA))], axis=1).astype(bf16)

    def weight_grad(left, h, l):
        both = dot(left, h, ((0,), (0,))) + dot(left, l, ((0,), (0,)))
        return both.reshape(D, 4, FQ).transpose(1, 0, 2)

    grads = jnp.stack([weight_grad(toks, gh, gl), weight_grad(toks, uh, ul), weight_grad(cots, hh, hl)], axis=1)
    back, mine = scatter(dx.reshape(HOT, CAP, WIDE), grads.reshape(192, 2, 64, FQ))
    out = jnp.dot(taking, back.reshape(rows, WIDE), preferred_element_type=f32).astype(bf16)
    return (out[:, :D], out[:, D], mine[0][None], mine[1][None], mine[2][None])


def solution(mesh):
    rows = P(("dp", "expert"), None)
    placed = (rows, rows, rows, P(("dp", "expert")), P("expert", None, None), P("expert", None, None),
              P("expert", None, None))
    return jax.shard_map(
        shards,
        mesh=mesh,
        in_specs=placed,
        out_specs=(rows, P(("dp", "expert")), P("expert", "dp", None), P("expert", "dp", None),
                   P("expert", "dp", None)),
        check_vma=False,
    )
```

time: 727 us -> 238 us (0.33); the launches traced: 715 us -> 236 us
  waiting for transfers between devices: 573 us -> 0 us
  Pallas kernels: 0 us -> 139 us
  starting transfers between devices: 53.7 us -> 0 us
  local copies, waits for them, and re-layouts: 11.2 us -> 35.9 us
  matrix products: 52.6 us -> 28.3 us
  other arithmetic: 9.56 us -> 32.7 us
  between operations: 14.7 us -> 0.92 us
    reduce_scatter x1 -> x0, waiting for transfers between devices: 415 us -> none  [shards(): reduced = lax.psum_scatter(stacked, 'dp', scatter_dimension=1, tiled=True)]
    all_to_all x5 -> x0, waiting for transfers between devices: 159 us -> none  [the longest x1 80.2 us: shards(): lax.all_to_all(send_tok, 'expert', split_axis=0, concat_axis=0, tiled=True)]
    pallas_call x0 -> x2, Pallas kernels: none -> 139 us  [the longest x1 71.6 us: gather(): pl.pallas_call(gather_kernel, out_shape=[jax.ShapeDtypeStruct(slot_tok.sh...]
    all_to_all x5 -> x0, starting transfers between devices: 53.4 us -> none  [the longest x1 16.2 us: shards(): lax.all_to_all(send_prob, 'expert', split_axis=0, concat_axis=0, tiled=True)]
    dot_general x10 -> x22, matrix products: 52.6 us -> 28.3 us  [the longest x18 25.3 us: dot(): return lax.dot_general(a, b, (dims, ((), ())), preferred_element_type=f32)]
    reshape x1 -> x3, local copies, waits for them, and re-layouts: 0.08 us -> 16.1 us  [weight_grad(): return both.reshape(D, 4, FQ).transpose(1, 0, 2)]
    shift_right_arithmetic x0 -> x1, other arithmetic: none -> 8.69 us  [shards(): wall >> 16]
    another operation x2, other arithmetic: 2.05 us -> 10 us  [the longest x1 10 us: shards(): jnp.stack([weight_grad(toks, gh, gl), weight_grad(toks, uh, ul), weight_g...]
  transfers between devices with their start and end apart: 6 -> 0, of which waited for: 4 -> 0; matrix products, arithmetic and copies ran while one was open for 8% -> 0% of each run, Pallas kernels for 0% -> 0%
where the time goes in v1:
time: 238 us; the launch traced here: 236 us
  Pallas kernels  139 us (58%)
  local copies, waits for them, and re-layouts  35.9 us (15%)
  other arithmetic  32.7 us (14%)
  matrix products  28.3 us (12%)
    pallas_call x1, Pallas kernels, gather(): pl.pallas_call(gather_kernel, out_shape=[jax.ShapeDtypeStruct(slot_tok.sh...  71.6 us
    pallas_call x1, Pallas kernels, scatter(): pl.pallas_call(scatter_kernel, out_shape=[jax.ShapeDtypeStruct(dx.shape,...  66.9 us
    dot_general x18, matrix products, dot(): return lax.dot_general(a, b, (dims, ((), ())), preferred_element_type=f32)  25.3 us
    reshape x3, local copies, waits for them, and re-layouts, weight_grad(): return both.reshape(D, 4, FQ).transpose(1, 0, 2)  16.1 us
    another operation x1, other arithmetic, shards(): jnp.stack([weight_grad(toks, gh, gl), weight_grad(toks, uh, ul), weight_g...  10 us
    shift_right_arithmetic x1, other arithmetic, shards(): wall >> 16  8.69 us
    sub x1, local copies, waits for them, and re-layouts, shards(): (wall & 65535) - 32768  6.61 us
    shift_right_arithmetic x1, local copies, waits for them, and re-layouts, shards(): wall >> 16  6.52 us

profile of v1, /device:TPU:1, one launch (start us, length us, event | category | flops | bytes accessed | tf_op | source)
XLA Modules:
  0.0 236.4 jit_solution(228085186780410776)
XLA Ops:
  0.7 1.4 abs_reduce_fusion.2
  2.1 1.3 abs_reduce_fusion.1
  3.4 1.3 abs_reduce_fusion
  8.2 0.8 dynamic-slice_bitcast_fusion.2
  9.0 0.8 dynamic-slice_bitcast_fusion
  10.5 1.2 convolution_convert_fusion.2
  11.7 1.3 convolution_convert_fusion
  13.0 71.6 %shard_map.110 = (bf16[4,48,2176]{2,1,0:T(8,128)(2,1)}, bf16[4,48,2048]{2,1,0:T(8,128)(2,1)}, s32[12,1024,128]{2,1,0:T(8,128)}, f32[4,8,128]{2,1,0:T(8,128)}) custom-call(bf16[4,48,2176]{2,1,0:T(8,128)(2,1)} %bitcast.129, bf16[4,48,2048]{2,1,0:T(8,128)(2,1)} %bitcast.130, s32[3,32,128]{2,1,0:T(8,128)} %fusion.51.w_ref, f32[8,128]{1,0:T(8,128)} %pad.4.s_ref), custom_call_target="tpu_custom_call" | custom-call | tf_op jit(solution)/shard_map/pallas_call | solution.py:148
  85.3 0.8 slice_convert_fusion
  86.2 8.7 %broadcast_shift-right-arithmetic_fusion = (s32[12,1024,128]{2,1,0:T(8,128)}, s32[12,1024,128]{2,1,0:T(8,128)}) fusion(s32[12,1024,128]{2,1,0:T(8,128)} %get-tuple-element.13), kind=kLoop, calls=%fused_computation.11 | loop fusion | flops 4718592 | bytes 18874368 | tf_op jit(solution)/shard_map/shift_right_arithmetic | solution.py:346
  94.9 6.5 %copy.16 = s32[4,3,1024,128]{2,3,0,1:T(8,128)} copy(s32[4,3,1024,128]{3,2,1,0:T(8,128)} %bitcast.109) | data formatting | bytes 12582912 | tf_op jit(solution)/shard_map/shift_right_arithmetic | solution.py:346
  101.4 6.6 %copy.17 = s32[4,3,1024,128]{2,3,0,1:T(8,128)} copy(s32[4,3,1024,128]{3,2,1,0:T(8,128)} %bitcast.107) | data formatting | bytes 12582912 | tf_op jit(solution)/shard_map/sub | solution.py:346
  108.0 6.4 %reduce-precision_convert_fusion = (bf16[3,2048,512]{1,2,0:T(8,128)(2,1)S(1)}, bf16[3,2048,512]{1,2,0:T(8,128)(2,1)S(1)}) fusion(s32[3,1024,512]{1,2,0:T(8,128)} %bitcast.108, s32[3,1024,512]{1,2,0:T(8,128)} %bitcast.106), kind=kLoop, calls=%fused_computation.1 | loop fusion | flops 18874368 | bytes 25165824 | tf_op jit(solution)/shard_map/convert_element_type | solution.py:310
  114.4 0.9 fusion.5
  115.3 0.8 fusion.4
  116.2 0.9 fusion.12
  117.1 0.8 fusion.2
  117.9 0.8 fusion.14
  119.0 1.8 add_multiply_fusion
  121.0 2.3 fusion.7
  123.3 2.3 convolution_add_fusion.7
  126.8 2.2 convolution_add_fusion.4
  130.2 0.8 fusion.32
  131.0 2.8 %convolution_add_fusion = f32[2048,512]{0,1:T(8,128)} fusion(f32[2048,512]{0,1:T(8,128)S(1)} %fusion.32, bf16[192,2048]{1,0:T(8,128)(2,1)S(1)} %bitcast.128, f32[192]{0:T(256)S(1)} %bitcast.145, f32[192,512]{1,0:T(8,128)S(1)} %copy-done.8, f32[192,512]{1,0:T(8,128)S(1)} %copy-done.9), kind=kOutput, calls=%fused_computation.8 | convolution fusion | flops 404586496 | bytes 9962240 | tf_op jit(solution)/shard_map/dot_general | solution.py:314
  133.8 5.4 %copy.20 = f32[2048,4,128]{2,0,1:T(8,128)} copy(f32[2048,4,128]{0,2,1:T(8,128)} %bitcast.112) | data formatting | bytes 8388608 | tf_op jit(solution)/shard_map/reshape | solution.py:374
  140.0 2.7 %convolution_add_fusion.2 = f32[2048,512]{0,1:T(8,128)} fusion(f32[2048,512]{0,1:T(8,128)S(1)} %fusion.30, f32[192,512]{1,0:T(8,128)S(1)} %get-tuple-element.21, bf16[192,2176]{1,0:T(8,128)(2,1)S(1)} %bitcast.122), kind=kOutput, calls=%fused_computation.10 | convolution fusion | flops 403996672 | bytes 9568256 | tf_op jit(solution)/shard_map/dot_general | solution.py:314
  142.7 5.4 %copy.18 = f32[2048,4,128]{2,0,1:T(8,128)} copy(f32[2048,4,128]{0,2,1:T(8,128)} %bitcast.111) | data formatting | bytes 8388608 | tf_op jit(solution)/shard_map/reshape | solution.py:374
  148.8 2.7 %convolution_add_fusion.1 = f32[2048,512]{0,1:T(8,128)} fusion(f32[2048,512]{0,1:T(8,128)S(1)} %fusion.31, f32[192,512]{1,0:T(8,128)S(1)} %get-tuple-element.23, bf16[192,2176]{1,0:T(8,128)(2,1)S(1)} %bitcast.124), kind=kOutput, calls=%fused_computation.9 | convolution fusion | flops 403996672 | bytes 9568256 | tf_op jit(solution)/shard_map/dot_general | solution.py:314
  151.5 5.4 %copy.19 = f32[2048,4,128]{2,0,1:T(8,128)} copy(f32[2048,4,128]{0,2,1:T(8,128)} %bitcast.110) | data formatting | bytes 8388608 | tf_op jit(solution)/shard_map/reshape | solution.py:374
  156.9 10.0 %pad_maximum_fusion = f32[4,3,2048,128]{3,2,1,0:T(8,128)} fusion(f32[4,1,2048,128]{3,2,1,0:T(8,128)} %bitcast.113, f32[4,1,2048,128]{3,2,1,0:T(8,128)} %bitcast.115, f32[4,1,2048,128]{3,2,1,0:T(8,128)} %bitcast.114), kind=kLoop, calls=%fused_computation.4 | loop fusion | flops 6291456 | bytes 25165824 | tf_op jit(solution)/shard_map/stack | solution.py:376
  166.9 66.9 %shard_map.111 = (bf16[4,48,2176]{2,1,0:T(8,128)(2,1)S(1)}, f32[3,64,128]{2,1,0:T(8,128)S(1)}) custom-call(bf16[4,48,2176]{2,1,0:T(8,128)(2,1)S(1)} %pad_maximum_fusion.1.dx_ref, f32[192,2,64,128]{3,2,1,0:T(8,128)} %bitcast.105), custom_call_target="tpu_custom_call" | custom-call | tf_op jit(solution)/shard_map/pallas_call | solution.py:282
  234.9 0.8 slice.100
  (47 shorter events, 10.9 us)
Async XLA Ops:
  0.6 9.8 %copy-start = (bf16[128,2048]{1,0:T(8,128)(2,1)S(1)}, bf16[128,2048]{1,0:T(8,128)(2,1)}, u32[]{:S(2)}) copy-start(bf16[128,2048]{1,0:T(8,128)(2,1)} %param.8) | copy-start | bytes 1572868
  0.6 11.0 %copy-start.10 = (bf16[128,2048]{1,0:T(8,128)(2,1)S(1)}, bf16[128,2048]{1,0:T(8,128)(2,1)}, u32[]{:S(2)}) copy-start(bf16[128,2048]{1,0:T(8,128)(2,1)} %param.7) | copy-start | bytes 1572868
  108.0 6.4 %copy-start.5 = (bf16[4,48,2176]{2,1,0:T(8,128)(2,1)S(1)}, bf16[4,48,2176]{2,1,0:T(8,128)(2,1)}, u32[]{:S(2)}) copy-start(bf16[4,48,2176]{2,1,0:T(8,128)(2,1)} %get-tuple-element.11) | copy-start | bytes 2506756
  114.4 2.6 %copy-start.4 = (bf16[3,2048,512]{1,2,0:T(8,128)(2,1)}, bf16[3,2048,512]{1,2,0:T(8,128)(2,1)S(1)}, u32[]{:S(2)}) copy-start(bf16[3,2048,512]{1,2,0:T(8,128)(2,1)S(1)} %get-tuple-element.18) | copy-start | bytes 18874372
  114.4 4.5 %copy-start.2 = (bf16[3,2048,512]{1,2,0:T(8,128)(2,1)}, bf16[3,2048,512]{1,2,0:T(8,128)(2,1)S(1)}, u32[]{:S(2)}) copy-start(bf16[3,2048,512]{1,2,0:T(8,128)(2,1)S(1)} %get-tuple-element.17) | copy-start | bytes 18874372
  115.3 1.8 copy-start.6
  117.1 3.7 %copy-start.7 = (f32[192,512]{1,0:T(8,128)}, f32[192,512]{1,0:T(8,128)S(1)}, u32[]{:S(2)}) copy-start(f32[192,512]{1,0:T(8,128)S(1)} %fusion.12) | copy-start | bytes 1179652
  121.0 4.7 %copy-start.3 = (bf16[3,2048,512]{1,2,0:T(8,128)(2,1)S(1)}, bf16[3,2048,512]{1,2,0:T(8,128)(2,1)}, u32[]{:S(2)}) copy-start(bf16[3,2048,512]{1,2,0:T(8,128)(2,1)} %copy-done.2) | copy-start | bytes 18874372
  129.0 1.0 copy-start.8
  129.1 1.1 copy-start.9
  166.9 69.4 %copy-start.1 = (bf16[128,2048]{1,0:T(8,128)(2,1)S(1)}, bf16[128,2048]{1,0:T(8,128)(2,1)}, u32[]{:S(2)}) copy-start(bf16[128,2048]{1,0:T(8,128)(2,1)} %param.8) | copy-start | bytes 1572868

commit v2 on v0

v2 whole, which is shorter than its diff:
```python
import math

import jax
import jax.numpy as jnp
from jax import lax
from jax.experimental import pallas as pl
from jax.experimental.pallas import tpu as pltpu
from jax.sharding import PartitionSpec as P

D = 2048
HOT = 4
CAP = 48
FQ = 128
NX, NYL, NYH, NZ, NC = 4, 4, 2, 8, 2
NY = NYL * NYH
EXTRA = 128
ROWS = HOT * CAP
PAIR = 2 * FQ
WIDE = D + EXTRA
W_TOP = 32767.0
MESH = pl.DeviceIdType.MESH
f32, bf16, i32 = jnp.float32, jnp.bfloat16, jnp.int32


def coords():
    dp = lax.axis_index("dp")
    ex = lax.axis_index("expert")
    core = lax.rem(dp, NC)
    x = lax.rem(lax.div(dp, NC), NX)
    ylo = lax.div(dp, NC * NX)
    yhi = lax.rem(ex, NYH)
    z = lax.div(ex, NYH)
    return x, yhi * NYL + ylo, z, core


def device(x, y, z, core):
    return ((lax.rem(y, NYL) * NX + x) * NC + core, z * NYH + lax.div(y, NYL))


def slot_route(z, k):
    odd = lax.rem(z, 2)
    sign = 1 - 2 * odd
    to = sign * (k if k % 2 == 0 else -k)
    come = sign * -k
    return lax.rem(z + to + NZ, NZ), lax.rem(z + come + NZ, NZ)


def remote(src, dst, send, recv, dev):
    return pltpu.make_async_remote_copy(
        src_ref=src, dst_ref=dst, send_sem=send, recv_sem=recv, device_id=dev, device_id_type=MESH
    )


def enter(sources, count):
    barrier = pltpu.get_barrier_semaphore()
    for dev in sources:
        pl.semaphore_signal(barrier, inc=1, device_id=dev, device_id_type=MESH)
    pl.semaphore_wait(barrier, count)


def dot(a, b, dims):
    return lax.dot_general(a, b, (dims, ((), ())), preferred_element_type=f32)


def halves(v):
    hi = v.astype(bf16)
    return hi, (v - hi.astype(f32)).astype(bf16)


def layer_kernel(tok_ref, cot_ref, w_ref, s_ref, back_ref, out_ref,
                 rtok, rcot, wall, sall, whi, wlo, dhi, dlo, shi, slo, dxb, gprob,
                 g, c_in, x_out, x_in, x_mid, total, y_out, y_in, z_out, z_in,
                 s_send, s_recv, t_send, t_recv, wz_send, wz_recv, wy_send, wy_recv, wx_send, wx_recv, wc_send, wc_recv,
                 r_send, r_recv, c_send, c_recv, x_send, x_recv, y_send, y_recv, z_send, z_recv, loc):
    x, y, z, c = coords()
    ylo, yhi = lax.rem(y, NYL), lax.div(y, NYL)
    zlo = lax.rem(z, 2)
    zp = z + 1 - 2 * zlo
    right, left = lax.rem(x + 1, NX), lax.rem(x + NX - 1, NX)
    far = lax.rem(x + 2, NX)
    routes = [slot_route(z, k) for k in (1, 2, 3)]
    ys = [lax.rem(y + j, NY) for j in range(1, NY)]
    to_dev = [device(x, y, to, c) for to, _ in routes]
    come_dev = [device(x, y, come, c) for _, come in routes]
    pair_dev = device(x, y, zp, c)
    y_dev = [device(x, yy, z, c) for yy in ys]
    right_dev, left_dev, core_dev = device(right, y, z, c), device(left, y, z, c), device(x, y, z, 1 - c)
    enter([to_dev[0], to_dev[1], come_dev[1], to_dev[2], pair_dev] + y_dev + [right_dev, left_dev, core_dev], 15)

    row = pl.multiple_of(((c * NX + x) * NYL + ylo) * 32, 32)
    quarter = yhi * 2 + zlo
    mine = wall.at[pl.ds(quarter * 3, 3), pl.ds(row, 32), :]
    wz = remote(w_ref, mine, wz_send, wz_recv, pair_dev)
    wz.start()
    sz = remote(s_ref, sall.at[quarter], s_send.at[0], s_recv.at[0], pair_dev)
    sz.start()
    locals_ = [
        pltpu.make_async_copy(w_ref, mine, loc.at[0]),
        pltpu.make_async_copy(s_ref, sall.at[quarter], loc.at[1]),
        pltpu.make_async_copy(tok_ref.at[pl.ds(0, CAP)], rtok.at[pl.ds(0, CAP)], loc.at[2]),
        pltpu.make_async_copy(cot_ref.at[pl.ds(0, CAP)], rcot.at[pl.ds(0, CAP)], loc.at[3]),
    ]
    for copy in locals_:
        copy.start()
    tokens = []
    for i, k in enumerate((1, 2, 3)):
        for j, (src, dst) in enumerate(((tok_ref, rtok), (cot_ref, rcot))):
            at = pl.ds(k * CAP, CAP)
            copy = remote(src.at[at], dst.at[at], t_send.at[i, j], t_recv.at[i, j], to_dev[i])
            copy.start()
            tokens.append(copy)
    for copy in locals_:
        copy.wait()
    wz.wait()
    sz.wait()
    block = wall.at[pl.ds(yhi * 6, 6), pl.ds(row, 32), :]
    wys = [remote(block, block, wy_send.at[j], wy_recv.at[j], y_dev[j]) for j in range(7)]
    for copy in wys:
        copy.start()
    both = sall.at[pl.ds(yhi * 2, 2)]
    sy = remote(both, both, s_send.at[1], s_recv.at[1], y_dev[3])
    sy.start()
    for copy in wys:
        copy.wait()
    sy.wait()

    def part(xx, lo, n):
        return wall.at[pl.ds(lo, n), pl.ds(pl.multiple_of((c * NX + xx) * 128, 128), 128), :]

    to_right = remote(part(x, 0, 12), part(x, 0, 12), wx_send.at[0], wx_recv.at[0], right_dev)
    to_left = remote(part(x, 0, 12), part(x, 0, 12), wx_send.at[1], wx_recv.at[1], left_dev)
    to_right.start()
    to_left.start()
    to_right.wait_recv()
    on_right = remote(part(left, 0, 6), part(left, 0, 6), wx_send.at[2], wx_recv.at[2], right_dev)
    on_right.start()
    to_left.wait_recv()
    on_left = remote(part(right, 6, 6), part(right, 6, 6), wx_send.at[3], wx_recv.at[3], left_dev)
    on_left.start()
    on_right.wait_recv()
    on_left.wait_recv()
    half = wall.at[:, pl.ds(pl.multiple_of(c * 512, 512), 512), :]
    wc = remote(half, half, wc_send, wc_recv, core_dev)
    wc.start()

    def unpack(base):
        def step(t, _):
            mp, at = lax.div(t, 4), pl.multiple_of(base + lax.rem(t, 4) * 128, 128)
            p, m = lax.div(mp, 3), lax.rem(mp, 3)
            for q in range(2):
                v = wall[(p * 2 + q) * 3 + m, pl.ds(at, 128), :]
                for start, u in ((0, v >> 16), (D // 2, (v & 65535) - 32768)):
                    hi, lo = halves(u.astype(f32))
                    whi[mp, pl.ds(pl.multiple_of(start + at, 128), 128), q * FQ:(q + 1) * FQ] = hi
                    wlo[mp, pl.ds(pl.multiple_of(start + at, 128), 128), q * FQ:(q + 1) * FQ] = lo
            return 0

        lax.fori_loop(0, 24, step, 0)

    unpack(c * 512)
    wc.wait_recv()
    unpack((1 - c) * 512)
    for copy in tokens:
        copy.wait_recv()

    gprob[...] = jnp.zeros_like(gprob)

    def forward(p, _):
        def pre(left, m):
            step = jnp.concatenate([sall[p * 2, pl.ds(m, 1), :], sall[p * 2 + 1, pl.ds(m, 1), :]], axis=1)
            both = dot(left, whi[p * 3 + m], ((1,), (0,))) + dot(left, wlo[p * 3 + m], ((1,), (0,)))
            return both * step, step

        toks = rtok[:, :D]
        gate_pre, gate_step = pre(toks, 0)
        up_pre, up_step = pre(toks, 1)
        backward, _ = pre(rcot[...], 2)
        pr = rtok[:, D:].astype(f32)
        pr = jnp.concatenate([pr, pr], axis=1)
        sig = jax.nn.sigmoid(gate_pre)
        act = gate_pre * sig
        hidden = act * up_pre
        gprob[...] += jnp.broadcast_to(jnp.sum(hidden * backward, axis=1, keepdims=True), (ROWS, EXTRA))
        d_hidden = pr * backward
        d_up = d_hidden * act
        d_gate = d_hidden * up_pre * sig * (1.0 + gate_pre * (1.0 - sig))
        for m, v in enumerate((d_gate, d_up, pr * hidden)):
            hi, lo = halves(v)
            dhi[p * 3 + m] = hi
            dlo[p * 3 + m] = lo
        for m, v in enumerate((d_gate * gate_step, d_up * up_step)):
            hi, lo = halves(v)
            shi[p * 2 + m] = hi
            slo[p * 2 + m] = lo
        return 0

    lax.fori_loop(0, 2, forward, 0)

    def weight_grad(m, left):
        def step(n, _):
            lt = left[:, pl.ds(pl.multiple_of(n * 256, 256), 256)]
            for p in range(2):
                v = dot(lt, dhi[p * 3 + m], ((0,), (0,))) + dot(lt, dlo[p * 3 + m], ((0,), (0,)))
                for q in range(2):
                    for i in range(4):
                        g[m, (p * 2 + q) * 16 + n * 2 + i // 2, i % 2] = v[i * 64:(i + 1) * 64, q * FQ:(q + 1) * FQ]
            return 0

        lax.fori_loop(0, 8, step, 0)

    def core_start(m):
        copy = remote(g.at[m, :, 1 - c], c_in.at[m], c_send.at[m], c_recv.at[m], core_dev)
        copy.start()
        return copy

    def acc(m, gq, xx):
        return g[m, gq * NX + xx, c] + c_in[m, gq * NX + xx]

    def x_first(m):
        def fill_far(i, _):
            x_out[m, 0, i] = acc(m, i, far).astype(bf16)
            return 0

        lax.fori_loop(0, 16, fill_far, 0)
        fr = remote(x_out.at[m, 0, pl.ds(0, 8)], x_mid.at[m, pl.ds(0, 8)], x_send.at[m, 0], x_recv.at[m, 0], right_dev)
        fl = remote(x_out.at[m, 0, pl.ds(8, 8)], x_mid.at[m, pl.ds(8, 8)], x_send.at[m, 1], x_recv.at[m, 1], left_dev)
        fr.start()
        fl.start()

        def fill_plain(i, _):
            x_out[m, 2, i] = acc(m, 8 + i, right).astype(bf16)
            x_out[m, 3, i] = acc(m, i, left).astype(bf16)
            return 0

        lax.fori_loop(0, 8, fill_plain, 0)
        pr = remote(x_out.at[m, 2, pl.ds(0, 8)], x_in.at[m, 0, pl.ds(8, 8)], x_send.at[m, 2], x_recv.at[m, 2], right_dev)
        pl_ = remote(x_out.at[m, 3, pl.ds(0, 8)], x_in.at[m, 1, pl.ds(0, 8)], x_send.at[m, 3], x_recv.at[m, 3], left_dev)
        pr.start()
        pl_.start()
        return [fr, fl, pr, pl_]

    def x_second(m, first):
        first[0].wait_recv()
        first[1].wait_recv()

        def fill_near(i, _):
            x_out[m, 1, i] = (acc(m, i, right) + x_mid[m, i].astype(f32)).astype(bf16)
            x_out[m, 1, 8 + i] = (acc(m, 8 + i, left) + x_mid[m, 8 + i].astype(f32)).astype(bf16)
            return 0

        lax.fori_loop(0, 8, fill_near, 0)
        sr = remote(x_out.at[m, 1, pl.ds(0, 8)], x_in.at[m, 0, pl.ds(0, 8)], x_send.at[m, 4], x_recv.at[m, 4], right_dev)
        sl = remote(x_out.at[m, 1, pl.ds(8, 8)], x_in.at[m, 1, pl.ds(8, 8)], x_send.at[m, 5], x_recv.at[m, 5], left_dev)
        sr.start()
        sl.start()
        return first + [sr, sl]

    def y_start(m, xs):
        for copy in xs[2:]:
            copy.wait_recv()

        def fill(i, _):
            v = acc(m, i, x) + x_in[m, 0, i].astype(f32) + x_in[m, 1, i].astype(f32)
            total[m, i] = v
            y_out[m, lax.div(i, 8), lax.rem(lax.div(i, 4), 2), lax.rem(i, 4)] = v.astype(bf16)
            return 0

        lax.fori_loop(0, 16, fill, 0)
        copies = []
        for j in range(7):
            src = y_out.at[m, lax.div(ys[j], NYL), :, lax.rem(ys[j], NYL)]
            copies.append(remote(src, y_in.at[m, j], y_send.at[m, j], y_recv.at[m, j], y_dev[j]))
            copies[-1].start()
        return copies

    def z_start(m, ycs):
        for copy in ycs:
            copy.wait_recv()

        def fill(i, _):
            v = total[m, (yhi * 2 + i) * NYL + ylo]
            for j in range(7):
                v = v + y_in[m, j, i].astype(f32)
            z_out[m, i] = v
            return 0

        lax.fori_loop(0, 2, fill, 0)
        copy = remote(z_out.at[m, 1 - zlo], z_in.at[m], z_send.at[m], z_recv.at[m], pair_dev)
        copy.start()
        return copy

    weight_grad(2, rcot)
    c2 = core_start(2)
    weight_grad(0, rtok)
    c0 = core_start(0)
    c2.wait_recv()
    x2 = x_first(2)
    weight_grad(1, rtok)
    c1 = core_start(1)
    c0.wait_recv()
    x0 = x_first(0)

    def input_grad(n, _):
        at = pl.ds(pl.multiple_of(n * 256, 256), 256)
        v = jnp.zeros((ROWS, 256), f32)
        for p in range(2):
            for m in range(2):
                hi, lo = whi[p * 3 + m, at, :], wlo[p * 3 + m, at, :]
                v += dot(shi[p * 2 + m], hi, ((1,), (1,)))
                v += dot(shi[p * 2 + m], lo, ((1,), (1,)))
                v += dot(slo[p * 2 + m], hi, ((1,), (1,)))
        dxb[:, at] = v.astype(bf16)
        return 0

    lax.fori_loop(0, 8, input_grad, 0)
    dxb[:, D:] = gprob[...].astype(bf16)
    returns = []
    for i, k in enumerate((1, 2, 3)):
        at = pl.ds(k * CAP, CAP)
        returns.append(remote(dxb.at[at], back_ref.at[at], r_send.at[i], r_recv.at[i], come_dev[i]))
        returns[-1].start()
    own = pltpu.make_async_copy(dxb.at[pl.ds(0, CAP)], back_ref.at[pl.ds(0, CAP)], loc.at[4])
    own.start()
    x2 = x_second(2, x2)
    c1.wait_recv()
    x1 = x_first(1)
    x0 = x_second(0, x0)
    y2 = y_start(2, x2)
    x1 = x_second(1, x1)
    y0 = y_start(0, x0)
    z2 = z_start(2, y2)
    y1 = y_start(1, x1)
    z0 = z_start(0, y0)
    z1 = z_start(1, y1)
    scale = 1.0 / math.sqrt(NX * NY * NZ * NC * 128)
    for m, copy in ((2, z2), (0, z0), (1, z1)):
        copy.wait_recv()
        out_ref[m] = (z_out[m, zlo] + z_in[m]) * scale
    for copy in returns:
        copy.wait()
    own.wait()
    for copy in tokens + [to_right, to_left, on_right, on_left, wc, c0, c1, c2] + x0 + x1 + x2 + y0 + y1 + y2 + [z0, z1, z2]:
        copy.wait_send()


def layer(slot_tok, slot_cot, packed, steps):
    vmem = pl.BlockSpec(memory_space=pltpu.VMEM)
    dma = pltpu.SemaphoreType.DMA
    V = pltpu.VMEM
    return pl.pallas_call(
        layer_kernel,
        out_shape=[
            jax.ShapeDtypeStruct((ROWS, WIDE), bf16),
            jax.ShapeDtypeStruct((3, 64, FQ), f32),
        ],
        in_specs=[vmem] * 4,
        out_specs=[vmem] * 2,
        scratch_shapes=[
            V((ROWS, WIDE), bf16), V((ROWS, D), bf16), V((12, D // 2, FQ), i32), V((4, 8, FQ), f32),
            V((6, D, PAIR), bf16), V((6, D, PAIR), bf16),
            V((6, ROWS, PAIR), bf16), V((6, ROWS, PAIR), bf16), V((4, ROWS, PAIR), bf16), V((4, ROWS, PAIR), bf16),
            V((ROWS, WIDE), bf16), V((ROWS, EXTRA), f32),
            V((3, 64, 2, 64, FQ), f32), V((3, 64, 64, FQ), f32),
            V((3, 4, 16, 64, FQ), bf16), V((3, 2, 16, 64, FQ), bf16), V((3, 16, 64, FQ), bf16),
            V((3, 16, 64, FQ), f32), V((3, 2, 2, 4, 64, FQ), bf16), V((3, 7, 2, 64, FQ), bf16),
            V((3, 2, 64, FQ), f32), V((3, 64, FQ), f32),
            dma((2,)), dma((2,)), dma((3, 2)), dma((3, 2)), dma, dma, dma((7,)), dma((7,)), dma((4,)), dma((4,)), dma, dma,
            dma((3,)), dma((3,)), dma((3,)), dma((3,)), dma((3, 6)), dma((3, 6)), dma((3, 7)), dma((3, 7)),
            dma((3,)), dma((3,)), dma((5,)),
        ],
        compiler_params=pltpu.CompilerParams(
            collective_id=0, has_side_effects=True, vmem_limit_bytes=62 * 1024 * 1024
        ),
    )(slot_tok, slot_cot, packed, steps)


def shards(tokens, cotangent, route, prob, w_gate, w_up, w_down):
    x, y, z, c = coords()
    odd = lax.rem(z, 2)
    turn = lax.rem(route[:, 0] - lax.div(z, 2) + HOT, HOT)
    slot = jnp.where(turn == 0, 0, jnp.where(turn == 1, 2 - odd, jnp.where(turn == 2, 3, 1 + odd)))
    onehot = (slot[:, None] == jnp.arange(HOT, dtype=jnp.int32)[None, :]).astype(f32)
    before = (jnp.arange(128)[:, None] > jnp.arange(128)[None, :]).astype(bf16)
    earlier = jnp.dot(before, onehot.astype(bf16), preferred_element_type=f32)
    rank = jnp.sum(earlier * onehot, axis=1).astype(jnp.int32)
    position = slot * CAP + rank
    placing = (jnp.arange(HOT * CAP, dtype=jnp.int32)[:, None] == position[None, :]).astype(bf16)
    taking = (position[:, None] == jnp.arange(HOT * CAP, dtype=jnp.int32)[None, :]).astype(bf16)
    wide = jnp.concatenate([tokens, jnp.broadcast_to(prob[:, None], (128, EXTRA))], axis=1)
    slot_tok = jnp.dot(placing, wide, preferred_element_type=f32).astype(bf16)
    slot_cot = jnp.dot(placing, cotangent, preferred_element_type=f32).astype(bf16)
    row = ((c * NX + x) * NYL + lax.rem(y, NYL)) * 32
    tops = [jnp.maximum(jnp.max(jnp.abs(w[0]), axis=0), 1e-30) for w in (w_gate, w_up, w_down)]
    steps = jnp.stack([t * (1.0 / W_TOP) for t in tops])
    chunk = jnp.stack([lax.dynamic_slice(w[0].reshape(2, D // 2, FQ), (0, row, 0), (2, 32, FQ))
                       for w in (w_gate, w_up, w_down)])
    units = jnp.clip(jnp.round(chunk / steps[:, None, None, :]), -W_TOP, W_TOP).astype(i32)
    packed = units[:, 0] * 65536 + (units[:, 1] + 32768)
    back, mine = layer(slot_tok, slot_cot, packed, jnp.pad(steps, ((0, 5), (0, 0))))
    out = jnp.dot(taking, back, preferred_element_type=f32).astype(bf16)
    return (out[:, :D], out[:, D], mine[0][None], mine[1][None], mine[2][None])


def solution(mesh):
    rows = P(("dp", "expert"), None)
    placed = (rows, rows, rows, P(("dp", "expert")), P("expert", None, None), P("expert", None, None),
              P("expert", None, None))
    return jax.shard_map(
        shards,
        mesh=mesh,
        in_specs=placed,
        out_specs=(rows, P(("dp", "expert")), P("expert", "dp", None), P("expert", "dp", None),
                   P("expert", "dp", None)),
        check_vma=False,
    )
```

time: 727 us -> 134 us (0.18)
  the two profiles are of different devices: /device:TPU:1 before, /device:TPU:8 now
where the time goes in v2:
time: 134 us
  Pallas kernels  122 us (91%)
  matrix products  4.24 us (3%)
  local copies, waits for them, and re-layouts  4.18 us (3%)
  other arithmetic  2.35 us (2%)
    pallas_call x1, Pallas kernels, layer(): pl.pallas_call(layer_kernel, out_shape=[jax.ShapeDtypeStruct((ROWS, WIDE)...  122 us

profile of v2, /device:TPU:8, one launch (start us, length us, event | category | flops | bytes accessed | tf_op | source)
XLA Modules:
  0.0 133.8 jit_solution(11793032582512121604)
XLA Ops:
  0.6 0.0 copy-start
  0.6 0.0 copy-start.2
  0.7 0.0 copy-start.1
  0.7 1.5 %abs_reduce_fusion.2 = f32[128]{0:T(128)S(1)} fusion(f32[1,2048,128]{2,1,0:T(8,128)} %param.11), kind=kLoop, calls=%fused_computation.7 | loop fusion | flops 524160 | bytes 1049088 | tf_op jit(solution)/shard_map/reduce_max | solution.py:393
  2.2 0.1 copy-done.2
  2.2 0.0 copy-start.5
  2.2 0.0 copy-start.6
  2.2 0.1 abs_reduce_fusion.1
  2.3 0.2 copy-done.1
  2.6 0.1 abs_reduce_fusion
  2.6 0.0 copy-start.3
  2.7 0.3 copy-done.5
  3.0 0.1 fusion
  3.2 0.6 pad.4.s_ref
  3.8 0.0 copy-done.6
  3.8 0.1 broadcast_in_dim.35
  3.9 0.8 dynamic-slice_bitcast_fusion.2
  4.7 0.6 fusion.9.w_ref
  5.3 0.0 copy-done
  5.3 1.3 convolution_convert_fusion.2.cot_ref
  6.6 0.0 copy-done.3
  6.6 1.3 convolution_convert_fusion.tok_ref
  7.9 122.2 %shard_map.110 = (bf16[192,2176]{1,0:T(8,128)(2,1)}, f32[3,64,128]{2,1,0:T(8,128)}) custom-call(bf16[192,2176]{1,0:T(8,128)(2,1)} %convolution_convert_fusion.tok_ref, bf16[192,2048]{1,0:T(8,128)(2,1)} %convolution_convert_fusion.2.cot_ref, s32[3,32,128]{2,1,0:T(8,128)} %fusion.9.w_ref, f32[8,128]{1,0:T(8,128)} %pad.4.s_ref), custom_call_target="tpu_custom_call" | custom-call | tf_op jit(solution)/shard_map/pallas_call | solution.py:350
  130.1 0.0 copy-start.4
  130.1 1.6 %convolution_convert_fusion.1 = bf16[128,2176]{1,0:T(8,128)(2,1)S(1)} fusion(bf16[192,2176]{1,0:T(8,128)(2,1)} %get-tuple-element.7, s32[128]{0:T(128)S(1)} %fusion.17), kind=kOutput, calls=%fused_computation.1 | convolution fusion | flops 107257856 | bytes 1393152 | tf_op jit(solution)/shard_map/dot_general | solution.py:400
  131.6 0.6 slice_reduce_fusion
  132.3 0.8 slice.30
  133.1 0.0 copy-done.4
  133.1 0.6 fusion.19
  (8 shorter events, 0.1 us)
Async XLA Ops:
  0.6 4.7 %copy-start = (bf16[128,2048]{1,0:T(8,128)(2,1)S(1)}, bf16[128,2048]{1,0:T(8,128)(2,1)}, u32[]{:S(2)}) copy-start(bf16[128,2048]{1,0:T(8,128)(2,1)} %param.8) | copy-start | bytes 1572868
  0.6 1.6 %copy-start.2 = (f32[1,2048,128]{2,1,0:T(8,128)S(1)}, f32[1,2048,128]{2,1,0:T(8,128)}, u32[]{:S(2)}) copy-start(f32[1,2048,128]{2,1,0:T(8,128)} %param.12) | copy-start | bytes 3145732
  0.7 1.9 %copy-start.1 = (f32[1,2048,128]{2,1,0:T(8,128)S(1)}, f32[1,2048,128]{2,1,0:T(8,128)}, u32[]{:S(2)}) copy-start(f32[1,2048,128]{2,1,0:T(8,128)} %param.13) | copy-start | bytes 3145732
  2.2 0.7 copy-start.5
  2.2 1.5 %copy-start.6 = (bf16[128]{0:T(256)(128)(2,1)S(1)}, bf16[128]{0:T(256)(128)(2,1)}, u32[]{:S(2)}) copy-start(bf16[128]{0:T(256)(128)(2,1)} %param.10) | copy-start | bytes 772
  2.6 3.9 %copy-start.3 = (bf16[128,2048]{1,0:T(8,128)(2,1)S(1)}, bf16[128,2048]{1,0:T(8,128)(2,1)}, u32[]{:S(2)}) copy-start(bf16[128,2048]{1,0:T(8,128)(2,1)} %param.7) | copy-start | bytes 1572868
  130.1 3.0 %copy-start.4 = (f32[3,64,128]{2,1,0:T(8,128)S(1)}, f32[3,64,128]{2,1,0:T(8,128)}, u32[]{:S(2)}) copy-start(f32[3,64,128]{2,1,0:T(8,128)} %get-tuple-element.8) | copy-start | bytes 294916

commit v3 on v2

v3 whole, which is shorter than its diff:
```python
import math

import jax
import jax.numpy as jnp
from jax import lax
from jax.experimental import pallas as pl
from jax.experimental.pallas import tpu as pltpu
from jax.sharding import PartitionSpec as P

D = 2048
HOT = 4
CAP = 48
FQ = 128
NX, NYL, NYH, NZ, NC = 4, 4, 2, 8, 2
NY = NYL * NYH
EXTRA = 128
ROWS = HOT * CAP
PAIR = 2 * FQ
WIDE = D + EXTRA
W_TOP = 32767.0
MESH = pl.DeviceIdType.MESH
f32, bf16, i32 = jnp.float32, jnp.bfloat16, jnp.int32


def coords():
    dp = lax.axis_index("dp")
    ex = lax.axis_index("expert")
    core = lax.rem(dp, NC)
    x = lax.rem(lax.div(dp, NC), NX)
    ylo = lax.div(dp, NC * NX)
    yhi = lax.rem(ex, NYH)
    z = lax.div(ex, NYH)
    return x, yhi * NYL + ylo, z, core


def device(x, y, z, core):
    return ((lax.rem(y, NYL) * NX + x) * NC + core, z * NYH + lax.div(y, NYL))


def slot_route(z, k):
    odd = lax.rem(z, 2)
    sign = 1 - 2 * odd
    to = sign * (k if k % 2 == 0 else -k)
    come = sign * -k
    return lax.rem(z + to + NZ, NZ), lax.rem(z + come + NZ, NZ)


def remote(src, dst, send, recv, dev):
    return pltpu.make_async_remote_copy(
        src_ref=src, dst_ref=dst, send_sem=send, recv_sem=recv, device_id=dev, device_id_type=MESH
    )


def enter(sources, count):
    barrier = pltpu.get_barrier_semaphore()
    for dev in sources:
        pl.semaphore_signal(barrier, inc=1, device_id=dev, device_id_type=MESH)
    pl.semaphore_wait(barrier, count)


def dot(a, b, dims):
    return lax.dot_general(a, b, (dims, ((), ())), preferred_element_type=f32)


def halves(v):
    hi = v.astype(bf16)
    return hi, (v - hi.astype(f32)).astype(bf16)


def layer_kernel(tok_ref, cot_ref, w_ref, s_ref, back_ref, out_ref,
                 rtok, rcot, wall, sall, whi, wlo, dhi, dlo, shi, slo, dxb, gprob,
                 g, c_in, x_out, x_in, x_mid, y_own, y_out, y_in, z_out, z_in,
                 s_send, s_recv, t_send, t_recv, wz_send, wz_recv, wy_send, wy_recv, wx_send, wx_recv, wc_send, wc_recv,
                 r_send, r_recv, c_send, c_recv, x_send, x_recv, y_send, y_recv, z_send, z_recv, loc):
    x, y, z, c = coords()
    ylo, yhi = lax.rem(y, NYL), lax.div(y, NYL)
    zlo = lax.rem(z, 2)
    zp = z + 1 - 2 * zlo
    right, left = lax.rem(x + 1, NX), lax.rem(x + NX - 1, NX)
    far = lax.rem(x + 2, NX)
    routes = [slot_route(z, k) for k in (1, 2, 3)]
    ys = [lax.rem(y + j, NY) for j in range(1, NY)]
    to_dev = [device(x, y, to, c) for to, _ in routes]
    come_dev = [device(x, y, come, c) for _, come in routes]
    pair_dev = device(x, y, zp, c)
    y_dev = [device(x, yy, z, c) for yy in ys]
    right_dev, left_dev, core_dev = device(right, y, z, c), device(left, y, z, c), device(x, y, z, 1 - c)
    enter([to_dev[0], to_dev[1], come_dev[1], to_dev[2], pair_dev] + y_dev + [right_dev, left_dev, core_dev], 15)

    quarter = yhi * 2 + zlo
    up_dev, down_dev = y_dev[0], y_dev[6]

    def rows_at(start, n):
        return pl.ds(pl.multiple_of(start, 16), n)

    def y0_block(yy, lo, n):
        return wall.at[pl.ds(lax.div(yy, NYL) * 6 + lo, n), rows_at(((c * NX + x) * NYL + lax.rem(yy, NYL)) * 16, 16), :]

    def x0_block(xx, lo, n):
        return wall.at[pl.ds(lo, n), rows_at((c * NX + xx) * 64, 64), :]

    def x1_block(xx, lo, n):
        return wall.at[pl.ds(yhi * 6 + lo, n), rows_at(512 + ((c * NYL + ylo) * NX + xx) * 16, 16), :]

    def y1_block(yy, lo, n):
        return wall.at[pl.ds(lax.div(yy, NYL) * 6 + lo, n), rows_at(512 + (c * NYL + lax.rem(yy, NYL)) * 64, 64), :]

    mine = [
        wall.at[pl.ds(quarter * 3, 3), rows_at(((c * NX + x) * NYL + ylo) * 16, 16), :],
        wall.at[pl.ds(quarter * 3, 3), rows_at(512 + ((c * NYL + ylo) * NX + x) * 16, 16), :],
    ]
    wz = [remote(w_ref.at[h], mine[h], wz_send.at[h], wz_recv.at[h], pair_dev) for h in range(2)]
    sz = remote(s_ref, sall.at[quarter], s_send.at[0], s_recv.at[0], pair_dev)
    for copy in wz + [sz]:
        copy.start()
    locals_ = [
        pltpu.make_async_copy(w_ref.at[0], mine[0], loc.at[0]),
        pltpu.make_async_copy(w_ref.at[1], mine[1], loc.at[5]),
        pltpu.make_async_copy(s_ref, sall.at[quarter], loc.at[1]),
        pltpu.make_async_copy(tok_ref.at[pl.ds(0, CAP)], rtok.at[pl.ds(0, CAP)], loc.at[2]),
        pltpu.make_async_copy(cot_ref.at[pl.ds(0, CAP)], rcot.at[pl.ds(0, CAP)], loc.at[3]),
    ]
    for copy in locals_:
        copy.start()
    tokens = []
    for i, k in enumerate((1, 2, 3)):
        for j, (src, dst) in enumerate(((tok_ref, rtok), (cot_ref, rcot))):
            at = pl.ds(k * CAP, CAP)
            copy = remote(src.at[at], dst.at[at], t_send.at[i, j], t_recv.at[i, j], to_dev[i])
            copy.start()
            tokens.append(copy)
    for copy in locals_:
        copy.wait()
    sent = []

    def start(src, send, recv, dev):
        copy = remote(src, src, send, recv, dev)
        copy.start()
        sent.append(copy)
        return copy

    def y_hop(block, h, d, whole):
        back, ahead = lax.rem(y - d + NY, NY), lax.rem(y + d, NY)
        first, second = (block(back, 0, 6), block(ahead, 0, 6)) if whole else (block(back, 0, 3), block(ahead, 3, 3))
        return [
            start(first, wy_send.at[h, 2 * d], wy_recv.at[h, 2 * d], up_dev),
            start(second, wy_send.at[h, 2 * d + 1], wy_recv.at[h, 2 * d + 1], down_dev),
        ]

    def x_hop(block, h, n):
        return [
            start(block(x, 0, n), wx_send.at[h, 0], wx_recv.at[h, 0], right_dev),
            start(block(x, 0, n), wx_send.at[h, 1], wx_recv.at[h, 1], left_dev),
        ]

    def x_relay(block, h, n):
        return [
            start(block(left, 0, n // 2), wx_send.at[h, 2], wx_recv.at[h, 2], right_dev),
            start(block(right, n // 2, n // 2), wx_send.at[h, 3], wx_recv.at[h, 3], left_dev),
        ]

    def arrived(copies):
        for copy in copies:
            copy.wait_recv()

    def core_send(h):
        return start(wall.at[:, rows_at(h * 512 + c * 256, 256), :], wc_send.at[h], wc_recv.at[h], core_dev)

    wz[0].wait()
    ya = y_hop(y0_block, 0, 0, True)
    wz[1].wait()
    xa = x_hop(x1_block, 1, 6)
    sz.wait()
    sy = start(sall.at[pl.ds(yhi * 2, 2)], s_send.at[1], s_recv.at[1], y_dev[3])
    arrived(ya)
    ya = y_hop(y0_block, 0, 1, True)
    arrived(xa)
    xa = x_relay(x1_block, 1, 6)
    arrived(ya)
    ya = y_hop(y0_block, 0, 2, True)
    arrived(xa)
    yb = y_hop(y1_block, 1, 0, True)
    arrived(ya)
    ya = y_hop(y0_block, 0, 3, False)
    arrived(ya)
    xb = x_hop(x0_block, 0, 12)
    arrived(yb)
    yb = y_hop(y1_block, 1, 1, True)
    arrived(xb)
    xb = x_relay(x0_block, 0, 12)
    arrived(yb)
    yb = y_hop(y1_block, 1, 2, True)
    arrived(xb)
    wc0 = core_send(0)

    def unpack(base):
        def step(t, _):
            mp, at = lax.div(t, 2), pl.multiple_of(base + lax.rem(t, 2) * 128, 128)
            p, m = lax.div(mp, 3), lax.rem(mp, 3)
            for q in range(2):
                v = wall[(q * 2 + p) * 3 + m, pl.ds(at, 128), :]
                for begin, u in ((0, v >> 16), (D // 2, (v & 65535) - 32768)):
                    hi, lo = halves(u.astype(f32))
                    whi[mp, pl.ds(pl.multiple_of(begin + at, 128), 128), q * FQ:(q + 1) * FQ] = hi
                    wlo[mp, pl.ds(pl.multiple_of(begin + at, 128), 128), q * FQ:(q + 1) * FQ] = lo
            return 0

        lax.fori_loop(0, 12, step, 0)

    arrived(yb)
    yb = y_hop(y1_block, 1, 3, False)
    unpack(c * 256)
    arrived(yb)
    wc1 = core_send(1)
    unpack(512 + c * 256)
    wc0.wait_recv()
    unpack((1 - c) * 256)
    wc1.wait_recv()
    unpack(512 + (1 - c) * 256)
    sy.wait_recv()
    arrived(tokens)

    gprob[...] = jnp.zeros_like(gprob)

    def forward(p):
        def pre(left, m):
            step = jnp.concatenate([sall[p, pl.ds(m, 1), :], sall[2 + p, pl.ds(m, 1), :]], axis=1)
            both = dot(left, whi[p * 3 + m], ((1,), (0,))) + dot(left, wlo[p * 3 + m], ((1,), (0,)))
            return both * step, step

        toks = rtok[:, :D]
        gate_pre, gate_step = pre(toks, 0)
        up_pre, up_step = pre(toks, 1)
        backward, _ = pre(rcot[...], 2)
        pr = rtok[:, D:].astype(f32)
        pr = jnp.concatenate([pr, pr], axis=1)
        sig = jax.nn.sigmoid(gate_pre)
        act = gate_pre * sig
        hidden = act * up_pre
        gprob[...] += jnp.broadcast_to(jnp.sum(hidden * backward, axis=1, keepdims=True), (ROWS, EXTRA))
        d_hidden = pr * backward
        d_up = d_hidden * act
        d_gate = d_hidden * up_pre * sig * (1.0 + gate_pre * (1.0 - sig))
        for m, v in enumerate((d_gate, d_up, pr * hidden)):
            hi, lo = halves(v)
            dhi[p * 3 + m] = hi
            dlo[p * 3 + m] = lo
        for m, v in enumerate((d_gate * gate_step, d_up * up_step)):
            hi, lo = halves(v)
            shi[p * 2 + m] = hi
            slo[p * 2 + m] = lo

    def weight_grad(p, m, left_ref):
        def step(n, _):
            lt = left_ref[:, pl.ds(pl.multiple_of(n * 256, 256), 256)]
            v = dot(lt, dhi[p * 3 + m], ((0,), (0,))) + dot(lt, dlo[p * 3 + m], ((0,), (0,)))
            for q in range(2):
                for i in range(4):
                    g[p * 3 + m, q * 16 + n * 2 + i // 2, i % 2] = v[i * 64:(i + 1) * 64, q * FQ:(q + 1) * FQ]
            return 0

        lax.fori_loop(0, 8, step, 0)
        copy = remote(g.at[p * 3 + m, :, 1 - c], c_in.at[p * 3 + m], c_send.at[p * 3 + m], c_recv.at[p * 3 + m], core_dev)
        copy.start()
        sent.append(copy)
        return copy

    def acc(k, yy, xx):
        return g[k, yy * NX + xx, c] + c_in[k, yy * NX + xx]

    def push(k, src, dst, n, dev):
        copy = remote(src, dst, x_send.at[k, n], x_recv.at[k, n], dev)
        copy.start()
        sent.append(copy)
        return copy

    first, second = pl.ds(0, 4), pl.ds(4, 4)

    def x_first(k, came):
        came.wait_recv()

        def fill_far(i, _):
            x_out[k, 0, i] = acc(k, i, far).astype(bf16)
            return 0

        lax.fori_loop(0, 8, fill_far, 0)
        fr = push(k, x_out.at[k, 0, first], x_mid.at[k, first], 0, right_dev)
        fl = push(k, x_out.at[k, 0, second], x_mid.at[k, second], 1, left_dev)

        def fill_plain(i, _):
            x_out[k, 2, i] = acc(k, 4 + i, right).astype(bf16)
            x_out[k, 3, i] = acc(k, i, left).astype(bf16)
            return 0

        lax.fori_loop(0, 4, fill_plain, 0)
        nr = push(k, x_out.at[k, 2, first], x_in.at[k, 0, second], 2, right_dev)
        nl = push(k, x_out.at[k, 3, first], x_in.at[k, 1, first], 3, left_dev)
        return [fr, fl], [nr, nl]

    def x_second(k, xs):
        arrived(xs[0])

        def fill_near(i, _):
            x_out[k, 1, i] = (acc(k, i, right) + x_mid[k, i].astype(f32)).astype(bf16)
            x_out[k, 1, 4 + i] = (acc(k, 4 + i, left) + x_mid[k, 4 + i].astype(f32)).astype(bf16)
            return 0

        lax.fori_loop(0, 4, fill_near, 0)
        return xs[1] + [
            push(k, x_out.at[k, 1, first], x_in.at[k, 0, first], 4, right_dev),
            push(k, x_out.at[k, 1, second], x_in.at[k, 1, second], 5, left_dev),
        ]

    def y_start(k, xs):
        arrived(xs)

        def total(i):
            return acc(k, i, x) + x_in[k, 0, i].astype(f32) + x_in[k, 1, i].astype(f32)

        def fill(i, _):
            y_out[k, i] = total(i).astype(bf16)
            return 0

        lax.fori_loop(0, 8, fill, 0)
        copies = [remote(y_out.at[k, ys[j]], y_in.at[k, j], y_send.at[k, j], y_recv.at[k, j], y_dev[j]) for j in range(7)]
        for copy in copies:
            copy.start()
        sent.extend(copies)
        y_own[k] = total(y)
        return copies

    def z_start(m, ycs):
        for p in range(2):
            arrived(ycs[p])
            v = y_own[p * 3 + m]
            for j in range(7):
                v = v + y_in[p * 3 + m, j].astype(f32)
            z_out[m, p] = v
        copy = remote(z_out.at[m, 1 - zlo], z_in.at[m], z_send.at[m], z_recv.at[m], pair_dev)
        copy.start()
        sent.append(copy)
        return copy

    def input_grad(n, _):
        at = pl.ds(pl.multiple_of(n * 256, 256), 256)
        v = jnp.zeros((ROWS, 256), f32)
        for p in range(2):
            for m in range(2):
                hi, lo = whi[p * 3 + m, at, :], wlo[p * 3 + m, at, :]
                v += dot(shi[p * 2 + m], hi, ((1,), (1,)))
                v += dot(shi[p * 2 + m], lo, ((1,), (1,)))
                v += dot(slo[p * 2 + m], hi, ((1,), (1,)))
        dxb[:, at] = v.astype(bf16)
        return 0

    forward(0)
    c02 = weight_grad(0, 2, rcot)
    c00 = weight_grad(0, 0, rtok)
    x02 = x_first(2, c02)
    c01 = weight_grad(0, 1, rtok)
    x00 = x_first(0, c00)
    forward(1)
    x02 = x_second(2, x02)
    x01 = x_first(1, c01)
    c12 = weight_grad(1, 2, rcot)
    x00 = x_second(0, x00)
    c10 = weight_grad(1, 0, rtok)
    y02 = y_start(2, x02)
    x01 = x_second(1, x01)
    x12 = x_first(5, c12)
    c11 = weight_grad(1, 1, rtok)
    y00 = y_start(0, x00)
    x10 = x_first(3, c10)
    lax.fori_loop(0, 4, input_grad, 0)
    x12 = x_second(5, x12)
    x11 = x_first(4, c11)
    y01 = y_start(1, x01)
    lax.fori_loop(4, 8, input_grad, 0)
    dxb[:, D:] = gprob[...].astype(bf16)
    returns = []
    for i, k in enumerate((1, 2, 3)):
        at = pl.ds(k * CAP, CAP)
        returns.append(remote(dxb.at[at], back_ref.at[at], r_send.at[i], r_recv.at[i], come_dev[i]))
        returns[-1].start()
    own = pltpu.make_async_copy(dxb.at[pl.ds(0, CAP)], back_ref.at[pl.ds(0, CAP)], loc.at[4])
    own.start()
    x10 = x_second(3, x10)
    y12 = y_start(5, x12)
    x11 = x_second(4, x11)
    y10 = y_start(3, x10)
    z2 = z_start(2, (y02, y12))
    y11 = y_start(4, x11)
    z0 = z_start(0, (y00, y10))
    z1 = z_start(1, (y01, y11))
    scale = 1.0 / math.sqrt(NX * NY * NZ * NC * 128)
    for m, copy in ((2, z2), (0, z0), (1, z1)):
        copy.wait_recv()
        out_ref[m] = (z_out[m, zlo] + z_in[m]) * scale
    for copy in returns:
        copy.wait()
    own.wait()
    for copy in tokens + sent:
        copy.wait_send()


def layer(slot_tok, slot_cot, packed, steps):
    vmem = pl.BlockSpec(memory_space=pltpu.VMEM)
    dma = pltpu.SemaphoreType.DMA
    V = pltpu.VMEM
    return pl.pallas_call(
        layer_kernel,
        out_shape=[
            jax.ShapeDtypeStruct((ROWS, WIDE), bf16),
            jax.ShapeDtypeStruct((3, 64, FQ), f32),
        ],
        in_specs=[vmem] * 4,
        out_specs=[vmem] * 2,
        scratch_shapes=[
            V((ROWS, WIDE), bf16), V((ROWS, D), bf16), V((12, D // 2, FQ), i32), V((4, 8, FQ), f32),
            V((6, D, PAIR), bf16), V((6, D, PAIR), bf16),
            V((6, ROWS, PAIR), bf16), V((6, ROWS, PAIR), bf16), V((4, ROWS, PAIR), bf16), V((4, ROWS, PAIR), bf16),
            V((ROWS, WIDE), bf16), V((ROWS, EXTRA), f32),
            V((6, 32, 2, 64, FQ), f32), V((6, 32, 64, FQ), f32),
            V((6, 4, 8, 64, FQ), bf16), V((6, 2, 8, 64, FQ), bf16), V((6, 8, 64, FQ), bf16),
            V((6, 64, FQ), f32), V((6, 8, 64, FQ), bf16), V((6, 7, 64, FQ), bf16),
            V((3, 2, 64, FQ), f32), V((3, 64, FQ), f32),
            dma((2,)), dma((2,)), dma((3, 2)), dma((3, 2)), dma((2,)), dma((2,)), dma((2, 8)), dma((2, 8)), dma((2, 4)),
            dma((2, 4)), dma((2,)), dma((2,)), dma((3,)), dma((3,)), dma((6,)), dma((6,)), dma((6, 6)), dma((6, 6)),
            dma((6, 7)), dma((6, 7)), dma((3,)), dma((3,)), dma((6,)),
        ],
        compiler_params=pltpu.CompilerParams(
            collective_id=0, has_side_effects=True, vmem_limit_bytes=62 * 1024 * 1024
        ),
    )(slot_tok, slot_cot, packed, steps)


def shards(tokens, cotangent, route, prob, w_gate, w_up, w_down):
    x, y, z, c = coords()
    odd = lax.rem(z, 2)
    turn = lax.rem(route[:, 0] - lax.div(z, 2) + HOT, HOT)
    slot = jnp.where(turn == 0, 0, jnp.where(turn == 1, 2 - odd, jnp.where(turn == 2, 3, 1 + odd)))
    onehot = (slot[:, None] == jnp.arange(HOT, dtype=jnp.int32)[None, :]).astype(f32)
    before = (jnp.arange(128)[:, None] > jnp.arange(128)[None, :]).astype(bf16)
    earlier = jnp.dot(before, onehot.astype(bf16), preferred_element_type=f32)
    rank = jnp.sum(earlier * onehot, axis=1).astype(jnp.int32)
    position = slot * CAP + rank
    placing = (jnp.arange(HOT * CAP, dtype=jnp.int32)[:, None] == position[None, :]).astype(bf16)
    taking = (position[:, None] == jnp.arange(HOT * CAP, dtype=jnp.int32)[None, :]).astype(bf16)
    wide = jnp.concatenate([tokens, jnp.broadcast_to(prob[:, None], (128, EXTRA))], axis=1)
    slot_tok = jnp.dot(placing, wide, preferred_element_type=f32).astype(bf16)
    slot_cot = jnp.dot(placing, cotangent, preferred_element_type=f32).astype(bf16)
    ylo = lax.rem(y, NYL)
    starts = (((c * NX + x) * NYL + ylo) * 16, 512 + ((c * NYL + ylo) * NX + x) * 16)
    weights = (w_gate, w_up, w_down)
    tops = [jnp.maximum(jnp.max(jnp.abs(w[0]), axis=0), 1e-30) for w in weights]
    steps = jnp.stack([t * (1.0 / W_TOP) for t in tops])
    chunk = jnp.stack([
        jnp.stack([lax.dynamic_slice(w[0].reshape(2, D // 2, FQ), (0, start, 0), (2, 16, FQ)) for w in weights])
        for start in starts
    ])
    units = jnp.clip(jnp.round(chunk / steps[None, :, None, None, :]), -W_TOP, W_TOP).astype(i32)
    packed = units[:, :, 0] * 65536 + (units[:, :, 1] + 32768)
    back, mine = layer(slot_tok, slot_cot, packed, jnp.pad(steps, ((0, 5), (0, 0))))
    out = jnp.dot(taking, back, preferred_element_type=f32).astype(bf16)
    return (out[:, :D], out[:, D], mine[0][None], mine[1][None], mine[2][None])


def solution(mesh):
    rows = P(("dp", "expert"), None)
    placed = (rows, rows, rows, P(("dp", "expert")), P("expert", None, None), P("expert", None, None),
              P("expert", None, None))
    return jax.shard_map(
        shards,
        mesh=mesh,
        in_specs=placed,
        out_specs=(rows, P(("dp", "expert")), P("expert", "dp", None), P("expert", "dp", None),
                   P("expert", "dp", None)),
        check_vma=False,
    )
```

time: 134 us -> 118 us (0.88)
  the two profiles are of different devices: /device:TPU:8 before, /device:TPU:64 now
where the time goes in v3:
time: 118 us; the launch traced here: 117 us
  Pallas kernels  106 us (90%)
  matrix products  4.23 us (4%)
  local copies, waits for them, and re-layouts  4.22 us (4%)
  other arithmetic  2.36 us (2%)
    pallas_call x1, Pallas kernels, layer(): pl.pallas_call(layer_kernel, out_shape=[jax.ShapeDtypeStruct((ROWS, WIDE)...  106 us

profile of v3, /device:TPU:64, one launch (start us, length us, event | category | flops | bytes accessed | tf_op | source)
XLA Modules:
  0.0 117.4 jit_solution(15690840973518517153)
XLA Ops:
  0.6 0.0 copy-start
  0.6 0.0 copy-start.2
  0.7 0.0 copy-start.1
  0.7 1.5 %abs_reduce_fusion.2 = f32[128]{0:T(128)S(1)} fusion(f32[1,2048,128]{2,1,0:T(8,128)} %param.11), kind=kLoop, calls=%fused_computation.7 | loop fusion | flops 524160 | bytes 1049088 | tf_op jit(solution)/shard_map/reduce_max | solution.py:455
  2.2 0.1 copy-done.2
  2.2 0.0 copy-start.5
  2.2 0.0 copy-start.6
  2.2 0.1 abs_reduce_fusion.1
  2.3 0.2 copy-done.1
  2.6 0.1 abs_reduce_fusion
  2.7 0.3 copy-done.5
  3.0 0.1 fusion
  3.2 0.6 pad.4.s_ref
  3.8 0.0 copy-done.6
  3.8 0.0 copy-start.3
  3.8 0.1 broadcast_in_dim.35
  3.9 0.8 dynamic-slice_bitcast_fusion.5
  4.7 0.6 fusion.9.w_ref
  5.4 0.0 copy-done
  5.4 1.3 %convolution_convert_fusion.2.cot_ref = bf16[192,2048]{1,0:T(8,128)(2,1)} fusion(bf16[128,2048]{1,0:T(8,128)(2,1)S(1)} %copy-done, s32[128]{0:T(128)S(1)} %fusion.14), kind=kOutput, calls=%fused_computation.2 | convolution fusion | flops 101081088 | bytes 1311232 | tf_op jit(solution)/shard_map/dot_general | solution.py:451
  6.6 0.0 copy-done.3
  6.6 1.3 %convolution_convert_fusion.tok_ref = bf16[192,2176]{1,0:T(8,128)(2,1)} fusion(bf16[128,128]{1,0:T(8,128)(2,1)S(1)} %broadcast_in_dim.35, bf16[128,2048]{1,0:T(8,128)(2,1)S(1)} %copy-done.3, s32[128]{0:T(128)S(1)} %fusion.14), kind=kOutput, calls=%fused_computation | convolution fusion | flops 108511232 | bytes 1393152 | tf_op jit(solution)/shard_map/dot_general | solution.py:450
  7.9 105.8 %shard_map.110 = (bf16[192,2176]{1,0:T(8,128)(2,1)}, f32[3,64,128]{2,1,0:T(8,128)}) custom-call(bf16[192,2176]{1,0:T(8,128)(2,1)} %convolution_convert_fusion.tok_ref, bf16[192,2048]{1,0:T(8,128)(2,1)} %convolution_convert_fusion.2.cot_ref, s32[2,3,16,128]{3,2,1,0:T(8,128)} %fusion.9.w_ref, f32[8,128]{1,0:T(8,128)} %pad.4.s_ref), custom_call_target="tpu_custom_call" | custom-call | tf_op jit(solution)/shard_map/pallas_call | solution.py:410
  113.8 0.0 copy-start.4
  113.8 1.5 %convolution_convert_fusion.1 = bf16[128,2176]{1,0:T(8,128)(2,1)S(1)} fusion(bf16[192,2176]{1,0:T(8,128)(2,1)} %get-tuple-element.7, s32[128]{0:T(128)S(1)} %fusion.17), kind=kOutput, calls=%fused_computation.1 | convolution fusion | flops 107257856 | bytes 1393152 | tf_op jit(solution)/shard_map/dot_general | solution.py:464
  115.3 0.6 slice_reduce_fusion
  115.9 0.8 slice.30
  116.8 0.0 copy-done.4
  116.8 0.6 fusion.19
  (10 shorter events, 0.1 us)
Async XLA Ops:
  0.6 4.7 %copy-start = (bf16[128,2048]{1,0:T(8,128)(2,1)S(1)}, bf16[128,2048]{1,0:T(8,128)(2,1)}, u32[]{:S(2)}) copy-start(bf16[128,2048]{1,0:T(8,128)(2,1)} %param.8) | copy-start | bytes 1572868
  0.6 1.6 %copy-start.2 = (f32[1,2048,128]{2,1,0:T(8,128)S(1)}, f32[1,2048,128]{2,1,0:T(8,128)}, u32[]{:S(2)}) copy-start(f32[1,2048,128]{2,1,0:T(8,128)} %param.12) | copy-start | bytes 3145732
  0.7 1.9 %copy-start.1 = (f32[1,2048,128]{2,1,0:T(8,128)S(1)}, f32[1,2048,128]{2,1,0:T(8,128)}, u32[]{:S(2)}) copy-start(f32[1,2048,128]{2,1,0:T(8,128)} %param.13) | copy-start | bytes 3145732
  2.2 0.7 copy-start.5
  2.2 1.5 %copy-start.6 = (bf16[128]{0:T(256)(128)(2,1)S(1)}, bf16[128]{0:T(256)(128)(2,1)}, u32[]{:S(2)}) copy-start(bf16[128]{0:T(256)(128)(2,1)} %param.10) | copy-start | bytes 772
  3.8 2.8 %copy-start.3 = (bf16[128,2048]{1,0:T(8,128)(2,1)S(1)}, bf16[128,2048]{1,0:T(8,128)(2,1)}, u32[]{:S(2)}) copy-start(bf16[128,2048]{1,0:T(8,128)(2,1)} %param.7) | copy-start | bytes 1572868
  113.8 3.0 %copy-start.4 = (f32[3,64,128]{2,1,0:T(8,128)S(1)}, f32[3,64,128]{2,1,0:T(8,128)}, u32[]{:S(2)}) copy-start(f32[3,64,128]{2,1,0:T(8,128)} %get-tuple-element.8) | copy-start | bytes 294916

commit v4 on v3

--- a/solution.py
+++ b/solution.py
@@ -51,10 +51,11 @@
     )
 
 
-def enter(sources, count):
+def enter(sources, count, meanwhile):
     barrier = pltpu.get_barrier_semaphore()
     for dev in sources:
         pl.semaphore_signal(barrier, inc=1, device_id=dev, device_id_type=MESH)
+    meanwhile()
     pl.semaphore_wait(barrier, count)
 
 
@@ -67,10 +68,10 @@
     return hi, (v - hi.astype(f32)).astype(bf16)
 
 
-def layer_kernel(tok_ref, cot_ref, w_ref, s_ref, back_ref, out_ref,
-                 rtok, rcot, wall, sall, whi, wlo, dhi, dlo, shi, slo, dxb, gprob,
+def layer_kernel(info_ref, tokens_ref, cots_ref, w_ref, s_ref, back_ref, backp_ref, out_ref,
+                 tok_ref, cot_ref, tok_t, cot_t, rtok, rcot, wall, sall, whi, wlo, dhi, dlo, shi, slo, dxb, dpb, gprob,
                  g, c_in, x_out, x_in, x_mid, y_own, y_out, y_in, z_out, z_in,
-                 s_send, s_recv, t_send, t_recv, wz_send, wz_recv, wy_send, wy_recv, wx_send, wx_recv, wc_send, wc_recv,
+                 s_send, s_recv, t_send, t_recv, wz_send, wz_recv, wd_send, wd_recv, wy_send, wy_recv, wx_send, wx_recv, wc_send, wc_recv,
                  r_send, r_recv, c_send, c_recv, x_send, x_recv, y_send, y_recv, z_send, z_recv, loc):
     x, y, z, c = coords()
     ylo, yhi = lax.rem(y, NYL), lax.div(y, NYL)
@@ -85,52 +86,56 @@
     pair_dev = device(x, y, zp, c)
     y_dev = [device(x, yy, z, c) for yy in ys]
     right_dev, left_dev, core_dev = device(right, y, z, c), device(left, y, z, c), device(x, y, z, 1 - c)
-    enter([to_dev[0], to_dev[1], come_dev[1], to_dev[2], pair_dev] + y_dev + [right_dev, left_dev, core_dev], 15)
-
-    quarter = yhi * 2 + zlo
+    def place():
+        here = lax.broadcasted_iota(jnp.int32, (ROWS, 128), 0).astype(f32) == info_ref[0:1, :]
+        prob = jnp.sum(jnp.where(here, info_ref[1:2, :], 0.0), axis=1, keepdims=True)
+        placing = here.astype(f32).astype(bf16)
+        tok_ref[:, :D] = dot(placing, tokens_ref[...], ((1,), (0,))).astype(bf16)
+        tok_ref[:, D:] = jnp.broadcast_to(prob, (ROWS, EXTRA)).astype(bf16)
+        cot_ref[...] = dot(placing, cots_ref[...], ((1,), (0,))).astype(bf16)
+
+    enter([to_dev[0], to_dev[1], come_dev[1], to_dev[2], pair_dev] + y_dev + [right_dev, left_dev, core_dev], 15, place)
+
     up_dev, down_dev = y_dev[0], y_dev[6]
 
     def rows_at(start, n):
         return pl.ds(pl.multiple_of(start, 16), n)
 
-    def y0_block(yy, lo, n):
-        return wall.at[pl.ds(lax.div(yy, NYL) * 6 + lo, n), rows_at(((c * NX + x) * NYL + lax.rem(yy, NYL)) * 16, 16), :]
-
-    def x0_block(xx, lo, n):
-        return wall.at[pl.ds(lo, n), rows_at((c * NX + xx) * 64, 64), :]
-
-    def x1_block(xx, lo, n):
-        return wall.at[pl.ds(yhi * 6 + lo, n), rows_at(512 + ((c * NYL + ylo) * NX + xx) * 16, 16), :]
-
-    def y1_block(yy, lo, n):
-        return wall.at[pl.ds(lax.div(yy, NYL) * 6 + lo, n), rows_at(512 + (c * NYL + lax.rem(yy, NYL)) * 64, 64), :]
-
-    mine = [
-        wall.at[pl.ds(quarter * 3, 3), rows_at(((c * NX + x) * NYL + ylo) * 16, 16), :],
-        wall.at[pl.ds(quarter * 3, 3), rows_at(512 + ((c * NYL + ylo) * NX + x) * 16, 16), :],
+    def y0_block(s, yy):
+        return wall.at[pl.ds(s * 6 + lax.div(yy, NYL) * 3, 3), rows_at(((c * NX + x) * NYL + lax.rem(yy, NYL)) * 16, 16), :]
+
+    def x0_block(s, xx, lo, n):
+        return wall.at[pl.ds(s * 6 + lo, n), rows_at((c * NX + xx) * 64, 64), :]
+
+    def x1_block(s, xx, lo, n):
+        return wall.at[pl.ds(s * 6 + yhi * 3 + lo, n), rows_at(512 + ((c * NYL + ylo) * NX + xx) * 16, 16), :]
+
+    def y1_block(s, yy, lo, n):
+        return wall.at[pl.ds(s * 6 + lax.div(yy, NYL) * 3, 3), rows_at(512 + (c * NYL + lax.rem(yy, NYL)) * 64 + lo, n), :]
+
+    mine = pl.ds((zlo * 2 + yhi) * 3, 3)
+    places = [
+        wall.at[mine, rows_at(((c * NX + x) * NYL + ylo) * 16, 16), :],
+        wall.at[mine, rows_at(512 + ((c * NYL + ylo) * NX + x) * 16, 16), :],
     ]
-    wz = [remote(w_ref.at[h], mine[h], wz_send.at[h], wz_recv.at[h], pair_dev) for h in range(2)]
-    sz = remote(s_ref, sall.at[quarter], s_send.at[0], s_recv.at[0], pair_dev)
+    wz = [remote(w_ref.at[h], places[h], wz_send.at[h], wz_recv.at[h], pair_dev) for h in range(2)]
+    sz = remote(s_ref, sall.at[zlo, yhi], s_send.at[0], s_recv.at[0], pair_dev)
     for copy in wz + [sz]:
         copy.start()
+    tokens = []
+    for j, (src, dst) in enumerate(((tok_ref, rtok), (cot_ref, rcot))):
+        for i, k in enumerate((3, 1, 2)):
+            at = pl.ds(k * CAP, CAP)
+            copy = remote(src.at[at], dst.at[at], t_send.at[i, j], t_recv.at[i, j], to_dev[k - 1])
+            copy.start()
+            tokens.append(copy)
     locals_ = [
-        pltpu.make_async_copy(w_ref.at[0], mine[0], loc.at[0]),
-        pltpu.make_async_copy(w_ref.at[1], mine[1], loc.at[5]),
-        pltpu.make_async_copy(s_ref, sall.at[quarter], loc.at[1]),
-        pltpu.make_async_copy(tok_ref.at[pl.ds(0, CAP)], rtok.at[pl.ds(0, CAP)], loc.at[2]),
-        pltpu.make_async_copy(cot_ref.at[pl.ds(0, CAP)], rcot.at[pl.ds(0, CAP)], loc.at[3]),
+        pltpu.make_async_copy(w_ref.at[0], places[0], loc.at[0]),
+        pltpu.make_async_copy(w_ref.at[1], places[1], loc.at[1]),
+        pltpu.make_async_copy(s_ref, sall.at[zlo, yhi], loc.at[2]),
     ]
     for copy in locals_:
         copy.start()
-    tokens = []
-    for i, k in enumerate((1, 2, 3)):
-        for j, (src, dst) in enumerate(((tok_ref, rtok), (cot_ref, rcot))):
-            at = pl.ds(k * CAP, CAP)
-            copy = remote(src.at[at], dst.at[at], t_send.at[i, j], t_recv.at[i, j], to_dev[i])
-            copy.start()
-            tokens.append(copy)
-    for copy in locals_:
-        copy.wait()
     sent = []
 
     def start(src, send, recv, dev):
@@ -139,66 +144,96 @@
         sent.append(copy)
         return copy
 
-    def y_hop(block, h, d, whole):
+    def y_direct(i, s):
+        return [start(y0_block(s, y), wd_send.at[i, j], wd_recv.at[i, j], y_dev[j]) for j in range(7)]
+
+    def y_hop(i, s, d):
         back, ahead = lax.rem(y - d + NY, NY), lax.rem(y + d, NY)
-        first, second = (block(back, 0, 6), block(ahead, 0, 6)) if whole else (block(back, 0, 3), block(ahead, 3, 3))
+        one, two = (y1_block(s, back, 0, 64), y1_block(s, ahead, 0, 64)) if d < 3 else (
+            y1_block(s, back, 0, 32), y1_block(s, ahead, 32, 32))
         return [
-            start(first, wy_send.at[h, 2 * d], wy_recv.at[h, 2 * d], up_dev),
-            start(second, wy_send.at[h, 2 * d + 1], wy_recv.at[h, 2 * d + 1], down_dev),
+            start(one, wy_send.at[i, 2 * d], wy_recv.at[i, 2 * d], up_dev),
+            start(two, wy_send.at[i, 2 * d + 1], wy_recv.at[i, 2 * d + 1], down_dev),
         ]
 
-    def x_hop(block, h, n):
+    def x_hop(block, i, s, n):
         return [
-            start(block(x, 0, n), wx_send.at[h, 0], wx_recv.at[h, 0], right_dev),
-            start(block(x, 0, n), wx_send.at[h, 1], wx_recv.at[h, 1], left_dev),
+            start(block(s, x, 0, n), wx_send.at[i, 0], wx_recv.at[i, 0], right_dev),
+            start(block(s, x, 0, n), wx_send.at[i, 1], wx_recv.at[i, 1], left_dev),
         ]
 
-    def x_relay(block, h, n):
+    def x_relay(block, i, s, n):
+        cut = n // 2
         return [
-            start(block(left, 0, n // 2), wx_send.at[h, 2], wx_recv.at[h, 2], right_dev),
-            start(block(right, n // 2, n // 2), wx_send.at[h, 3], wx_recv.at[h, 3], left_dev),
+            start(block(s, left, 0, cut), wx_send.at[i, 2], wx_recv.at[i, 2], right_dev),
+            start(block(s, right, cut, n - cut), wx_send.at[i, 3], wx_recv.at[i, 3], left_dev),
         ]
 
     def arrived(copies):
         for copy in copies:
             copy.wait_recv()
 
-    def core_send(h):
-        return start(wall.at[:, rows_at(h * 512 + c * 256, 256), :], wc_send.at[h], wc_recv.at[h], core_dev)
-
+    def core_send(i, h, s):
+        return start(wall.at[pl.ds(s * 6, 6), rows_at(h * 512 + c * 256, 256), :], wc_send.at[i], wc_recv.at[i], core_dev)
+
+    sa, sb = zlo, 1 - zlo
+    for copy in locals_:
+        copy.wait()
+    ya = y_direct(0, sa)
+    xa = x_hop(x1_block, 2, sa, 3)
     wz[0].wait()
-    ya = y_hop(y0_block, 0, 0, True)
+    yb = y_direct(1, sb)
     wz[1].wait()
-    xa = x_hop(x1_block, 1, 6)
+    xb = x_hop(x1_block, 3, sb, 3)
     sz.wait()
-    sy = start(sall.at[pl.ds(yhi * 2, 2)], s_send.at[1], s_recv.at[1], y_dev[3])
+    mates = sall.at[:, yhi]
+    sy = start(mates, s_send.at[1], s_recv.at[1], y_dev[3])
+    rtok[pl.ds(0, CAP), :] = tok_ref[pl.ds(0, CAP), :]
+    rcot[pl.ds(0, CAP), :] = cot_ref[pl.ds(0, CAP), :]
+
+    arrived(xa)
+    xa = x_relay(x1_block, 2, sa, 3)
+    arrived(xb)
+    xb = x_relay(x1_block, 3, sb, 3)
     arrived(ya)
-    ya = y_hop(y0_block, 0, 1, True)
+    x0a = x_hop(x0_block, 0, sa, 6)
     arrived(xa)
-    xa = x_relay(x1_block, 1, 6)
-    arrived(ya)
-    ya = y_hop(y0_block, 0, 2, True)
-    arrived(xa)
-    yb = y_hop(y1_block, 1, 0, True)
-    arrived(ya)
-    ya = y_hop(y0_block, 0, 3, False)
-    arrived(ya)
-    xb = x_hop(x0_block, 0, 12)
+    y1a = y_hop(0, sa, 0)
+    arrived(xb)
+    y1b = y_hop(1, sb, 0)
     arrived(yb)
-    yb = y_hop(y1_block, 1, 1, True)
-    arrived(xb)
-    xb = x_relay(x0_block, 0, 12)
-    arrived(yb)
-    yb = y_hop(y1_block, 1, 2, True)
-    arrived(xb)
-    wc0 = core_send(0)
+    x0b = x_hop(x0_block, 1, sb, 6)
+    arrived(y1a)
+    y1a = y_hop(0, sa, 1)
+    arrived(y1b)
+    y1b = y_hop(1, sb, 1)
+    arrived(x0a)
+    x0a = x_relay(x0_block, 0, sa, 6)
+    arrived(y1a)
+    y1a = y_hop(0, sa, 2)
+    arrived(y1b)
+    y1b = y_hop(1, sb, 2)
+    arrived(x0b)
+    x0b = x_relay(x0_block, 1, sb, 6)
+    arrived(x0a)
+    wcs = [core_send(0, 0, sa)]
+    arrived(y1a)
+    y1a = y_hop(0, sa, 3)
+    arrived(y1b)
+    y1b = y_hop(1, sb, 3)
+    arrived(x0b)
+    wcs.append(core_send(1, 0, sb))
+    arrived(y1a)
+    wcs.append(core_send(2, 1, sa))
+    arrived(y1b)
+    wcs.append(core_send(3, 1, sb))
 
     def unpack(base):
         def step(t, _):
             mp, at = lax.div(t, 2), pl.multiple_of(base + lax.rem(t, 2) * 128, 128)
             p, m = lax.div(mp, 3), lax.rem(mp, 3)
             for q in range(2):
-                v = wall[(q * 2 + p) * 3 + m, pl.ds(at, 128), :]
+                v = wall[(p * 2 + q) * 3 + m, pl.ds(at, 128), :]
                 for begin, u in ((0, v >> 16), (D // 2, (v & 65535) - 32768)):
                     hi, lo = halves(u.astype(f32))
                     whi[mp, pl.ds(pl.multiple_of(begin + at, 128), 128), q * FQ:(q + 1) * FQ] = hi
@@ -207,30 +242,37 @@
 
         lax.fori_loop(0, 12, step, 0)
 
-    arrived(yb)
-    yb = y_hop(y1_block, 1, 3, False)
     unpack(c * 256)
-    arrived(yb)
-    wc1 = core_send(1)
     unpack(512 + c * 256)
-    wc0.wait_recv()
+    arrived(tokens[:3])
+
+    def turn(left_ref, out_t):
+        def step(n, _):
+            at = pl.ds(pl.multiple_of(n * 256, 256), 256)
+            out_t[at, :] = jnp.transpose(left_ref[:, at])
+            return 0
+
+        lax.fori_loop(0, 8, step, 0)
+
+    turn(rtok, tok_t)
+    arrived(wcs)
     unpack((1 - c) * 256)
-    wc1.wait_recv()
     unpack(512 + (1 - c) * 256)
     sy.wait_recv()
-    arrived(tokens)
 
     gprob[...] = jnp.zeros_like(gprob)
 
     def forward(p):
         def pre(left, m):
-            step = jnp.concatenate([sall[p, pl.ds(m, 1), :], sall[2 + p, pl.ds(m, 1), :]], axis=1)
+            step = jnp.concatenate([sall[p, 0, pl.ds(m, 1), :], sall[p, 1, pl.ds(m, 1), :]], axis=1)
             both = dot(left, whi[p * 3 + m], ((1,), (0,))) + dot(left, wlo[p * 3 + m], ((1,), (0,)))
             return both * step, step
 
         toks = rtok[:, :D]
         gate_pre, gate_step = pre(toks, 0)
         up_pre, up_step = pre(toks, 1)
+        if p == 0:
+            arrived(tokens[3:])
         backward, _ = pre(rcot[...], 2)
         pr = rtok[:, D:].astype(f32)
         pr = jnp.concatenate([pr, pr], axis=1)
@@ -252,8 +294,8 @@
 
     def weight_grad(p, m, left_ref):
         def step(n, _):
-            lt = left_ref[:, pl.ds(pl.multiple_of(n * 256, 256), 256)]
-            v = dot(lt, dhi[p * 3 + m], ((0,), (0,))) + dot(lt, dlo[p * 3 + m], ((0,), (0,)))
+            lt = left_ref[pl.ds(pl.multiple_of(n * 256, 256), 256), :]
+            v = dot(lt, dhi[p * 3 + m], ((1,), (0,))) + dot(lt, dlo[p * 3 + m], ((1,), (0,)))
             for q in range(2):
                 for i in range(4):
                     g[p * 3 + m, q * 16 + n * 2 + i // 2, i % 2] = v[i * 64:(i + 1) * 64, q * FQ:(q + 1) * FQ]
@@ -353,37 +395,44 @@
         dxb[:, at] = v.astype(bf16)
         return 0
 
+    returns = []
+
+    def give(src, dst, n, lo, width):
+        for i, k in enumerate((3, 1, 2)):
+            at = (pl.ds(k * CAP, CAP), pl.ds(lo, width))
+            copy = remote(src.at[at], dst.at[at], r_send.at[n, i], r_recv.at[n, i], come_dev[k - 1])
+            copy.start()
+            returns.append(copy)
+        dst[pl.ds(0, CAP), lo:lo + width] = src[pl.ds(0, CAP), lo:lo + width]
+
     forward(0)
-    c02 = weight_grad(0, 2, rcot)
-    c00 = weight_grad(0, 0, rtok)
+    turn(rcot, cot_t)
+    c02 = weight_grad(0, 2, cot_t)
+    c00 = weight_grad(0, 0, tok_t)
+    forward(1)
     x02 = x_first(2, c02)
-    c01 = weight_grad(0, 1, rtok)
+    lax.fori_loop(0, 4, input_grad, 0)
+    give(dxb, back_ref, 0, 0, D // 2)
+    dpb[...] = gprob[...].astype(bf16)
+    give(dpb, backp_ref, 1, 0, EXTRA)
     x00 = x_first(0, c00)
-    forward(1)
+    c01 = weight_grad(0, 1, tok_t)
     x02 = x_second(2, x02)
+    lax.fori_loop(4, 8, input_grad, 0)
+    give(dxb, back_ref, 2, D // 2, D // 2)
     x01 = x_first(1, c01)
-    c12 = weight_grad(1, 2, rcot)
     x00 = x_second(0, x00)
-    c10 = weight_grad(1, 0, rtok)
+    c12 = weight_grad(1, 2, cot_t)
+    c10 = weight_grad(1, 0, tok_t)
+    x12 = x_first(5, c12)
     y02 = y_start(2, x02)
     x01 = x_second(1, x01)
-    x12 = x_first(5, c12)
-    c11 = weight_grad(1, 1, rtok)
+    c11 = weight_grad(1, 1, tok_t)
+    x10 = x_first(3, c10)
     y00 = y_start(0, x00)
-    x10 = x_first(3, c10)
-    lax.fori_loop(0, 4, input_grad, 0)
     x12 = x_second(5, x12)
     x11 = x_first(4, c11)
     y01 = y_start(1, x01)
-    lax.fori_loop(4, 8, input_grad, 0)
-    dxb[:, D:] = gprob[...].astype(bf16)
-    returns = []
-    for i, k in enumerate((1, 2, 3)):
-        at = pl.ds(k * CAP, CAP)
-        returns.append(remote(dxb.at[at], back_ref.at[at], r_send.at[i], r_recv.at[i], come_dev[i]))
-        returns[-1].start()
-    own = pltpu.make_async_copy(dxb.at[pl.ds(0, CAP)], back_ref.at[pl.ds(0, CAP)], loc.at[4])
-    own.start()
     x10 = x_second(3, x10)
     y12 = y_start(5, x12)
     x11 = x_second(4, x11)
@@ -392,46 +441,46 @@
     y11 = y_start(4, x11)
     z0 = z_start(0, (y00, y10))
     z1 = z_start(1, (y01, y11))
+    arrived(returns)
     scale = 1.0 / math.sqrt(NX * NY * NZ * NC * 128)
     for m, copy in ((2, z2), (0, z0), (1, z1)):
         copy.wait_recv()
         out_ref[m] = (z_out[m, zlo] + z_in[m]) * scale
-    for copy in returns:
-        copy.wait()
-    own.wait()
-    for copy in tokens + sent:
+    for copy in tokens + sent + returns:
         copy.wait_send()
 
 
-def layer(slot_tok, slot_cot, packed, steps):
+def layer(info, tokens, cots, packed, steps):
     vmem = pl.BlockSpec(memory_space=pltpu.VMEM)
     dma = pltpu.SemaphoreType.DMA
     V = pltpu.VMEM
     return pl.pallas_call(
         layer_kernel,
         out_shape=[
-            jax.ShapeDtypeStruct((ROWS, WIDE), bf16),
+            jax.ShapeDtypeStruct((ROWS, D), bf16),
+            jax.ShapeDtypeStruct((ROWS, EXTRA), bf16),
             jax.ShapeDtypeStruct((3, 64, FQ), f32),
         ],
-        in_specs=[vmem] * 4,
-        out_specs=[vmem] * 2,
+        in_specs=[vmem] * 5,
+        out_specs=[vmem] * 3,
         scratch_shapes=[
-            V((ROWS, WIDE), bf16), V((ROWS, D), bf16), V((12, D // 2, FQ), i32), V((4, 8, FQ), f32),
+            V((ROWS, WIDE), bf16), V((ROWS, D), bf16), V((D, ROWS), bf16), V((D, ROWS), bf16),
+            V((ROWS, WIDE), bf16), V((ROWS, D), bf16), V((12, D // 2, FQ), i32), V((2, 2, 8, FQ), f32),
             V((6, D, PAIR), bf16), V((6, D, PAIR), bf16),
             V((6, ROWS, PAIR), bf16), V((6, ROWS, PAIR), bf16), V((4, ROWS, PAIR), bf16), V((4, ROWS, PAIR), bf16),
-            V((ROWS, WIDE), bf16), V((ROWS, EXTRA), f32),
+            V((ROWS, D), bf16), V((ROWS, EXTRA), bf16), V((ROWS, EXTRA), f32),
             V((6, 32, 2, 64, FQ), f32), V((6, 32, 64, FQ), f32),
             V((6, 4, 8, 64, FQ), bf16), V((6, 2, 8, 64, FQ), bf16), V((6, 8, 64, FQ), bf16),
             V((6, 64, FQ), f32), V((6, 8, 64, FQ), bf16), V((6, 7, 64, FQ), bf16),
             V((3, 2, 64, FQ), f32), V((3, 64, FQ), f32),
-            dma((2,)), dma((2,)), dma((3, 2)), dma((3, 2)), dma((2,)), dma((2,)), dma((2, 8)), dma((2, 8)), dma((2, 4)),
-            dma((2, 4)), dma((2,)), dma((2,)), dma((3,)), dma((3,)), dma((6,)), dma((6,)), dma((6, 6)), dma((6, 6)),
-            dma((6, 7)), dma((6, 7)), dma((3,)), dma((3,)), dma((6,)),
+            dma((2,)), dma((2,)), dma((3, 2)), dma((3, 2)), dma((2,)), dma((2,)), dma((2, 7)), dma((2, 7)), dma((2, 8)), dma((2, 8)),
+            dma((4, 4)), dma((4, 4)), dma((4,)), dma((4,)), dma((3, 3)), dma((3, 3)), dma((6,)), dma((6,)), dma((6, 6)), dma((6, 6)),
+            dma((6, 7)), dma((6, 7)), dma((3,)), dma((3,)), dma((3,)),
         ],
         compiler_params=pltpu.CompilerParams(
             collective_id=0, has_side_effects=True, vmem_limit_bytes=62 * 1024 * 1024
         ),
-    )(slot_tok, slot_cot, packed, steps)
+    )(info, tokens, cots, packed, steps)
 
 
 def shards(tokens, cotangent, route, prob, w_gate, w_up, w_down):
@@ -444,11 +493,6 @@
     earlier = jnp.dot(before, onehot.astype(bf16), preferred_element_type=f32)
     rank = jnp.sum(earlier * onehot, axis=1).astype(jnp.int32)
     position = slot * CAP + rank
-    placing = (jnp.arange(HOT * CAP, dtype=jnp.int32)[:, None] == position[None, :]).astype(bf16)
-    taking = (position[:, None] == jnp.arange(HOT * CAP, dtype=jnp.int32)[None, :]).astype(bf16)
-    wide = jnp.concatenate([tokens, jnp.broadcast_to(prob[:, None], (128, EXTRA))], axis=1)
-    slot_tok = jnp.dot(placing, wide, preferred_element_type=f32).astype(bf16)
-    slot_cot = jnp.dot(placing, cotangent, preferred_element_type=f32).astype(bf16)
     ylo = lax.rem(y, NYL)
     starts = (((c * NX + x) * NYL + ylo) * 16, 512 + ((c * NYL + ylo) * NX + x) * 16)
     weights = (w_gate, w_up, w_down)
@@ -460,9 +504,12 @@
     ])
     units = jnp.clip(jnp.round(chunk / steps[None, :, None, None, :]), -W_TOP, W_TOP).astype(i32)
     packed = units[:, :, 0] * 65536 + (units[:, :, 1] + 32768)
-    back, mine = layer(slot_tok, slot_cot, packed, jnp.pad(steps, ((0, 5), (0, 0))))
-    out = jnp.dot(taking, back, preferred_element_type=f32).astype(bf16)
-    return (out[:, :D], out[:, D], mine[0][None], mine[1][None], mine[2][None])
+    info = jnp.stack([position.astype(f32), prob.astype(f32)] * 4)
+    back, back_prob, mine = layer(info, tokens, cotangent, packed, jnp.pad(steps, ((0, 5), (0, 0))))
+    taking = (position[:, None] == jnp.arange(ROWS, dtype=jnp.int32)[None, :]).astype(bf16)
+    grad_input = jnp.dot(taking, back, preferred_element_type=f32).astype(bf16)
+    grad_prob = jnp.dot(taking, back_prob, preferred_element_type=f32)[:, 0].astype(bf16)
+    return (grad_input, grad_prob, mine[0][None], mine[1][None], mine[2][None])
 
 
 def solution(mesh):

time: 118 us -> 113 us (0.958)
  the two profiles are of different devices: /device:TPU:64 before, /device:TPU:1 now
where the time goes in v4:
time: 113 us
  Pallas kernels  102 us (90%)
  local copies, waits for them, and re-layouts  3.88 us (3%)
  other arithmetic  3.03 us (3%)
  matrix products  2.72 us (2%)
    pallas_call x1, Pallas kernels, layer(): pl.pallas_call(layer_kernel, out_shape=[jax.ShapeDtypeStruct((ROWS, D), b...  102 us
    dot_general x1, matrix products, shards(): grad_input = jnp.dot(taking, back, preferred_element_type=f32).astype(bf16)  2.32 us

profile of v4, /device:TPU:1, one launch (start us, length us, event | category | flops | bytes accessed | tf_op | source)
XLA Modules:
  0.0 112.8 jit_solution(11494114193655488067)
XLA Ops:
  0.6 0.0 copy-start.1
  0.7 0.7 bitcast_convert_fusion
  1.4 0.0 copy-start
  1.4 1.4 %abs_reduce_fusion.2 = f32[128]{0:T(128)S(1)} fusion(f32[1,2048,128]{2,1,0:T(8,128)} %param.11), kind=kLoop, calls=%fused_computation.5 | loop fusion | flops 524160 | bytes 1049088 | tf_op jit(solution)/shard_map/reduce_max | solution.py:499
  2.8 0.0 copy-done.1
  2.8 0.1 abs_reduce_fusion.1
  2.9 0.1 copy-done
  3.0 0.1 abs_reduce_fusion
  3.1 0.0 copy-start.3
  3.2 0.6 copy-done.3
  3.8 0.1 fusion
  4.0 0.6 stack.57.info_ref
  4.6 0.6 pad.4.s_ref
  5.2 0.7 dynamic-slice_bitcast_fusion.5
  6.0 0.6 fusion.8.w_ref
  6.7 102.4 %shard_map.110 = (bf16[192,2048]{1,0:T(8,128)(2,1)}, bf16[192,128]{1,0:T(8,128)(2,1)}, f32[3,64,128]{2,1,0:T(8,128)}) custom-call(f32[8,128]{1,0:T(8,128)} %stack.57.info_ref, bf16[128,2048]{1,0:T(8,128)(2,1)} %tokens_ref.1, bf16[128,2048]{1,0:T(8,128)(2,1)} %cots_ref.1, s32[2,3,16,128]{3,2,1,0:T(8,128)} %fusion.8.w_ref, f32[8,128]{1,0:T(8,128)} %pad.4.s_ref), custom_call_target="tpu_custom_call" | custom-call | tf_op jit(solution)/shard_map/pallas_call | solution.py:457
  109.1 0.0 copy-start.4
  109.1 0.0 copy-start.2
  109.1 2.3 %convolution_convert_fusion = bf16[128,2048]{1,0:T(8,128)(2,1)} fusion(bf16[192,2048]{1,0:T(8,128)(2,1)} %get-tuple-element.8, s32[128]{0:T(128)S(1)} %fusion.15), kind=kOutput, calls=%fused_computation | convolution fusion | flops 100950016 | bytes 1311232 | tf_op jit(solution)/shard_map/dot_general | solution.py:510
  111.4 0.0 copy-done.4
  111.4 0.3 fusion.1
  111.7 0.5 fusion.14
  112.2 0.0 copy-done.2
  112.2 0.6 fusion.17
  (10 shorter events, 0.1 us)
Async XLA Ops:
  0.6 2.2 %copy-start.1 = (f32[1,2048,128]{2,1,0:T(8,128)S(1)}, f32[1,2048,128]{2,1,0:T(8,128)}, u32[]{:S(2)}) copy-start(f32[1,2048,128]{2,1,0:T(8,128)} %param.12) | copy-start | bytes 3145732
  1.4 1.6 %copy-start = (f32[1,2048,128]{2,1,0:T(8,128)S(1)}, f32[1,2048,128]{2,1,0:T(8,128)}, u32[]{:S(2)}) copy-start(f32[1,2048,128]{2,1,0:T(8,128)} %param.13) | copy-start | bytes 3145732
  3.1 0.7 copy-start.3
  109.1 2.3 %copy-start.4 = (bf16[192,128]{1,0:T(8,128)(2,1)S(1)}, bf16[192,128]{1,0:T(8,128)(2,1)}, u32[]{:S(2)}) copy-start(bf16[192,128]{1,0:T(8,128)(2,1)} %get-tuple-element.9) | copy-start | bytes 147460
  109.1 3.1 %copy-start.2 = (f32[3,64,128]{2,1,0:T(8,128)S(1)}, f32[3,64,128]{2,1,0:T(8,128)}, u32[]{:S(2)}) copy-start(f32[3,64,128]{2,1,0:T(8,128)} %get-tuple-element.10) | copy-start | bytes 294916

commit v5 on v4

--- a/solution.py
+++ b/solution.py
@@ -70,7 +70,7 @@
 
 def layer_kernel(info_ref, tokens_ref, cots_ref, w_ref, s_ref, back_ref, backp_ref, out_ref,
                  tok_ref, cot_ref, tok_t, cot_t, rtok, rcot, wall, sall, whi, wlo, dhi, dlo, shi, slo, dxb, dpb, gprob,
-                 g, c_in, x_out, x_in, x_mid, y_own, y_out, y_in, z_out, z_in,
+                 g, c_in, x_out, x_in, x_mid, y_own, y_out, y_in, z_out, z_in, f_out, f_in, f_send, f_recv,
                  s_send, s_recv, t_send, t_recv, wz_send, wz_recv, wd_send, wd_recv, wy_send, wy_recv, wx_send, wx_recv, wc_send, wc_recv,
                  r_send, r_recv, c_send, c_recv, x_send, x_recv, y_send, y_recv, z_send, z_recv, loc):
     x, y, z, c = coords()
@@ -319,7 +319,8 @@
     first, second = pl.ds(0, 4), pl.ds(4, 4)
 
     def x_first(k, came):
-        came.wait_recv()
+        if came is not None:
+            came.wait_recv()
 
         def fill_far(i, _):
             x_out[k, 0, i] = acc(k, i, far).astype(bf16)
@@ -395,6 +396,30 @@
         dxb[:, at] = v.astype(bf16)
         return 0
 
+    down, over_there = zlo * 3 + 2, (1 - zlo) * 3 + 2
+
+    def z_first(*came):
+        arrived(came)
+
+        def fill(i, _):
+            f_out[i] = (g[over_there, i, c] + c_in[over_there, i]).astype(bf16)
+            return 0
+
+        lax.fori_loop(0, 32, fill, 0)
+        copy = remote(f_out, f_in, f_send, f_recv, pair_dev)
+        copy.start()
+        sent.append(copy)
+        return copy
+
+    def z_join(copy):
+        copy.wait_recv()
+
+        def fill(i, _):
+            c_in[down, i] = c_in[down, i] + f_in[i].astype(f32)
+            return 0
+
+        lax.fori_loop(0, 32, fill, 0)
+
     returns = []
 
     def give(src, dst, n, lo, width):
@@ -407,45 +432,48 @@
 
     forward(0)
     turn(rcot, cot_t)
+    c00 = weight_grad(0, 0, tok_t)
+    c01 = weight_grad(0, 1, tok_t)
+    forward(1)
+    x00 = x_first(0, c00)
     c02 = weight_grad(0, 2, cot_t)
-    c00 = weight_grad(0, 0, tok_t)
-    forward(1)
-    x02 = x_first(2, c02)
+    c12 = weight_grad(1, 2, cot_t)
+    x01 = x_first(1, c01)
+    x00 = x_second(0, x00)
+    over = z_first(c02, c12)
+    c10 = weight_grad(1, 0, tok_t)
+    x01 = x_second(1, x01)
+    x10 = x_first(3, c10)
+    y00 = y_start(0, x00)
     lax.fori_loop(0, 4, input_grad, 0)
     give(dxb, back_ref, 0, 0, D // 2)
     dpb[...] = gprob[...].astype(bf16)
     give(dpb, backp_ref, 1, 0, EXTRA)
-    x00 = x_first(0, c00)
-    c01 = weight_grad(0, 1, tok_t)
-    x02 = x_second(2, x02)
+    c11 = weight_grad(1, 1, tok_t)
+    x10 = x_second(3, x10)
+    y01 = y_start(1, x01)
+    x11 = x_first(4, c11)
+    z_join(over)
+    x2 = x_first(down, None)
     lax.fori_loop(4, 8, input_grad, 0)
     give(dxb, back_ref, 2, D // 2, D // 2)
-    x01 = x_first(1, c01)
-    x00 = x_second(0, x00)
-    c12 = weight_grad(1, 2, cot_t)
-    c10 = weight_grad(1, 0, tok_t)
-    x12 = x_first(5, c12)
-    y02 = y_start(2, x02)
-    x01 = x_second(1, x01)
-    c11 = weight_grad(1, 1, tok_t)
-    x10 = x_first(3, c10)
-    y00 = y_start(0, x00)
-    x12 = x_second(5, x12)
-    x11 = x_first(4, c11)
-    y01 = y_start(1, x01)
-    x10 = x_second(3, x10)
-    y12 = y_start(5, x12)
     x11 = x_second(4, x11)
     y10 = y_start(3, x10)
-    z2 = z_start(2, (y02, y12))
+    x2 = x_second(down, x2)
     y11 = y_start(4, x11)
     z0 = z_start(0, (y00, y10))
+    y2 = y_start(down, x2)
     z1 = z_start(1, (y01, y11))
     arrived(returns)
     scale = 1.0 / math.sqrt(NX * NY * NZ * NC * 128)
-    for m, copy in ((2, z2), (0, z0), (1, z1)):
+    for m, copy in ((0, z0), (1, z1)):
         copy.wait_recv()
         out_ref[m] = (z_out[m, zlo] + z_in[m]) * scale
+    arrived(y2)
+    v = y_own[down]
+    for j in range(7):
+        v = v + y_in[down, j].astype(f32)
+    out_ref[2] = v * scale
     for copy in tokens + sent + returns:
         copy.wait_send()
 
@@ -472,7 +500,7 @@
             V((6, 32, 2, 64, FQ), f32), V((6, 32, 64, FQ), f32),
             V((6, 4, 8, 64, FQ), bf16), V((6, 2, 8, 64, FQ), bf16), V((6, 8, 64, FQ), bf16),
             V((6, 64, FQ), f32), V((6, 8, 64, FQ), bf16), V((6, 7, 64, FQ), bf16),
-            V((3, 2, 64, FQ), f32), V((3, 64, FQ), f32),
+            V((3, 2, 64, FQ), f32), V((3, 64, FQ), f32), V((32, 64, FQ), bf16), V((32, 64, FQ), bf16), dma, dma,
             dma((2,)), dma((2,)), dma((3, 2)), dma((3, 2)), dma((2,)), dma((2,)), dma((2, 7)), dma((2, 7)), dma((2, 8)), dma((2, 8)),
             dma((4, 4)), dma((4, 4)), dma((4,)), dma((4,)), dma((3, 3)), dma((3, 3)), dma((6,)), dma((6,)), dma((6, 6)), dma((6, 6)),
             dma((6, 7)), dma((6, 7)), dma((3,)), dma((3,)), dma((3,)),

time: 113 us -> 114 us (level)
  the two profiles are of different devices: /device:TPU:1 before, /device:TPU:16 now
where the time goes in v5:
time: 114 us
  Pallas kernels  104 us (91%)
  local copies, waits for them, and re-layouts  3.88 us (3%)
  other arithmetic  3.03 us (3%)
  matrix products  2.72 us (2%)
    pallas_call x1, Pallas kernels, layer(): pl.pallas_call(layer_kernel, out_shape=[jax.ShapeDtypeStruct((ROWS, D), b...  104 us
    dot_general x1, matrix products, shards(): grad_input = jnp.dot(taking, back, preferred_element_type=f32).astype(bf16)  2.32 us

profile of v5, /device:TPU:16, one launch (start us, length us, event | category | flops | bytes accessed | tf_op | source)
XLA Modules:
  0.0 114.0 jit_solution(7947110905906990864)
XLA Ops:
  0.6 0.0 copy-start.1
  0.7 0.7 bitcast_convert_fusion
  1.4 0.0 copy-start
  1.4 1.4 %abs_reduce_fusion.2 = f32[128]{0:T(128)S(1)} fusion(f32[1,2048,128]{2,1,0:T(8,128)} %param.11), kind=kLoop, calls=%fused_computation.5 | loop fusion | flops 524160 | bytes 1049088 | tf_op jit(solution)/shard_map/reduce_max | solution.py:527
  2.8 0.0 copy-done.1
  2.8 0.1 abs_reduce_fusion.1
  2.9 0.1 copy-done
  3.0 0.1 abs_reduce_fusion
  3.1 0.0 copy-start.3
  3.2 0.6 copy-done.3
  3.8 0.1 fusion
  4.0 0.6 stack.57.info_ref
  4.6 0.6 pad.4.s_ref
  5.2 0.7 dynamic-slice_bitcast_fusion.5
  6.0 0.6 fusion.8.w_ref
  6.7 103.6 %shard_map.110 = (bf16[192,2048]{1,0:T(8,128)(2,1)}, bf16[192,128]{1,0:T(8,128)(2,1)}, f32[3,64,128]{2,1,0:T(8,128)}) custom-call(f32[8,128]{1,0:T(8,128)} %stack.57.info_ref, bf16[128,2048]{1,0:T(8,128)(2,1)} %tokens_ref.1, bf16[128,2048]{1,0:T(8,128)(2,1)} %cots_ref.1, s32[2,3,16,128]{3,2,1,0:T(8,128)} %fusion.8.w_ref, f32[8,128]{1,0:T(8,128)} %pad.4.s_ref), custom_call_target="tpu_custom_call" | custom-call | tf_op jit(solution)/shard_map/pallas_call | solution.py:485
  110.2 0.0 copy-start.4
  110.2 0.0 copy-start.2
  110.2 2.3 %convolution_convert_fusion = bf16[128,2048]{1,0:T(8,128)(2,1)} fusion(bf16[192,2048]{1,0:T(8,128)(2,1)} %get-tuple-element.8, s32[128]{0:T(128)S(1)} %fusion.15), kind=kOutput, calls=%fused_computation | convolution fusion | flops 100950016 | bytes 1311232 | tf_op jit(solution)/shard_map/dot_general | solution.py:538
  112.6 0.0 copy-done.4
  112.6 0.3 fusion.1
  112.8 0.5 fusion.14
  113.3 0.0 copy-done.2
  113.3 0.6 fusion.17
  (10 shorter events, 0.1 us)
Async XLA Ops:
  0.6 2.2 %copy-start.1 = (f32[1,2048,128]{2,1,0:T(8,128)S(1)}, f32[1,2048,128]{2,1,0:T(8,128)}, u32[]{:S(2)}) copy-start(f32[1,2048,128]{2,1,0:T(8,128)} %param.12) | copy-start | bytes 3145732
  1.4 1.6 %copy-start = (f32[1,2048,128]{2,1,0:T(8,128)S(1)}, f32[1,2048,128]{2,1,0:T(8,128)}, u32[]{:S(2)}) copy-start(f32[1,2048,128]{2,1,0:T(8,128)} %param.13) | copy-start | bytes 3145732
  3.1 0.7 copy-start.3
  110.2 2.3 %copy-start.4 = (bf16[192,128]{1,0:T(8,128)(2,1)S(1)}, bf16[192,128]{1,0:T(8,128)(2,1)}, u32[]{:S(2)}) copy-start(bf16[192,128]{1,0:T(8,128)(2,1)} %get-tuple-element.9) | copy-start | bytes 147460
  110.2 3.1 %copy-start.2 = (f32[3,64,128]{2,1,0:T(8,128)S(1)}, f32[3,64,128]{2,1,0:T(8,128)}, u32[]{:S(2)}) copy-start(f32[3,64,128]{2,1,0:T(8,128)} %get-tuple-element.10) | copy-start | bytes 294916

commit v6 on v4

--- a/solution.py
+++ b/solution.py
@@ -409,24 +409,24 @@
     turn(rcot, cot_t)
     c02 = weight_grad(0, 2, cot_t)
     c00 = weight_grad(0, 0, tok_t)
+    x02 = x_first(2, c02)
     forward(1)
-    x02 = x_first(2, c02)
+    c01 = weight_grad(0, 1, tok_t)
+    x00 = x_first(0, c00)
+    x02 = x_second(2, x02)
+    c12 = weight_grad(1, 2, cot_t)
+    x01 = x_first(1, c01)
     lax.fori_loop(0, 4, input_grad, 0)
     give(dxb, back_ref, 0, 0, D // 2)
     dpb[...] = gprob[...].astype(bf16)
     give(dpb, backp_ref, 1, 0, EXTRA)
-    x00 = x_first(0, c00)
-    c01 = weight_grad(0, 1, tok_t)
-    x02 = x_second(2, x02)
-    lax.fori_loop(4, 8, input_grad, 0)
-    give(dxb, back_ref, 2, D // 2, D // 2)
-    x01 = x_first(1, c01)
     x00 = x_second(0, x00)
-    c12 = weight_grad(1, 2, cot_t)
     c10 = weight_grad(1, 0, tok_t)
     x12 = x_first(5, c12)
     y02 = y_start(2, x02)
     x01 = x_second(1, x01)
+    lax.fori_loop(4, 8, input_grad, 0)
+    give(dxb, back_ref, 2, D // 2, D // 2)
     c11 = weight_grad(1, 1, tok_t)
     x10 = x_first(3, c10)
     y00 = y_start(0, x00)

time: 113 us -> 112 us (level)
  no operation moved by 1% of the time
where the time goes in v6:
time: 112 us
  Pallas kernels  101 us (90%)
  local copies, waits for them, and re-layouts  3.88 us (3%)
  other arithmetic  3.03 us (3%)
  matrix products  2.72 us (2%)
    pallas_call x1, Pallas kernels, layer(): pl.pallas_call(layer_kernel, out_shape=[jax.ShapeDtypeStruct((ROWS, D), b...  101 us
    dot_general x1, matrix products, shards(): grad_input = jnp.dot(taking, back, preferred_element_type=f32).astype(bf16)  2.32 us

profile of v6, /device:TPU:1, one launch (start us, length us, event | category | flops | bytes accessed | tf_op | source)
XLA Modules:
  0.0 111.9 jit_solution(225119579872150324)
XLA Ops:
  0.6 0.0 copy-start.1
  0.7 0.7 bitcast_convert_fusion
  1.4 0.0 copy-start
  1.4 1.4 %abs_reduce_fusion.2 = f32[128]{0:T(128)S(1)} fusion(f32[1,2048,128]{2,1,0:T(8,128)} %param.11), kind=kLoop, calls=%fused_computation.5 | loop fusion | flops 524160 | bytes 1049088 | tf_op jit(solution)/shard_map/reduce_max | solution.py:499
  2.8 0.0 copy-done.1
  2.8 0.1 abs_reduce_fusion.1
  2.9 0.1 copy-done
  3.0 0.1 abs_reduce_fusion
  3.1 0.0 copy-start.3
  3.2 0.6 copy-done.3
  3.8 0.1 fusion
  4.0 0.6 stack.57.info_ref
  4.6 0.6 pad.4.s_ref
  5.2 0.7 dynamic-slice_bitcast_fusion.5
  6.0 0.6 fusion.8.w_ref
  6.7 101.5 %shard_map.110 = (bf16[192,2048]{1,0:T(8,128)(2,1)}, bf16[192,128]{1,0:T(8,128)(2,1)}, f32[3,64,128]{2,1,0:T(8,128)}) custom-call(f32[8,128]{1,0:T(8,128)} %stack.57.info_ref, bf16[128,2048]{1,0:T(8,128)(2,1)} %tokens_ref.1, bf16[128,2048]{1,0:T(8,128)(2,1)} %cots_ref.1, s32[2,3,16,128]{3,2,1,0:T(8,128)} %fusion.8.w_ref, f32[8,128]{1,0:T(8,128)} %pad.4.s_ref), custom_call_target="tpu_custom_call" | custom-call | tf_op jit(solution)/shard_map/pallas_call | solution.py:457
  108.1 0.0 copy-start.4
  108.2 0.0 copy-start.2
  108.2 2.3 %convolution_convert_fusion = bf16[128,2048]{1,0:T(8,128)(2,1)} fusion(bf16[192,2048]{1,0:T(8,128)(2,1)} %get-tuple-element.8, s32[128]{0:T(128)S(1)} %fusion.15), kind=kOutput, calls=%fused_computation | convolution fusion | flops 100950016 | bytes 1311232 | tf_op jit(solution)/shard_map/dot_general | solution.py:510
  110.5 0.0 copy-done.4
  110.5 0.3 fusion.1
  110.7 0.5 fusion.14
  111.2 0.0 copy-done.2
  111.3 0.6 fusion.17
  (10 shorter events, 0.1 us)
Async XLA Ops:
  0.6 2.2 %copy-start.1 = (f32[1,2048,128]{2,1,0:T(8,128)S(1)}, f32[1,2048,128]{2,1,0:T(8,128)}, u32[]{:S(2)}) copy-start(f32[1,2048,128]{2,1,0:T(8,128)} %param.12) | copy-start | bytes 3145732
  1.4 1.6 %copy-start = (f32[1,2048,128]{2,1,0:T(8,128)S(1)}, f32[1,2048,128]{2,1,0:T(8,128)}, u32[]{:S(2)}) copy-start(f32[1,2048,128]{2,1,0:T(8,128)} %param.13) | copy-start | bytes 3145732
  3.1 0.7 copy-start.3
  108.1 2.3 %copy-start.4 = (bf16[192,128]{1,0:T(8,128)(2,1)S(1)}, bf16[192,128]{1,0:T(8,128)(2,1)}, u32[]{:S(2)}) copy-start(bf16[192,128]{1,0:T(8,128)(2,1)} %get-tuple-element.9) | copy-start | bytes 147460
  108.2 3.1 %copy-start.2 = (f32[3,64,128]{2,1,0:T(8,128)S(1)}, f32[3,64,128]{2,1,0:T(8,128)}, u32[]{:S(2)}) copy-start(f32[3,64,128]{2,1,0:T(8,128)} %get-tuple-element.10) | copy-start | bytes 294916
